TPU v7x, 256 devices: a whole 4x4x8 slice. The times are simulated.
256 devices in a mesh: sector: 64 (over z, x, y_hi), band: 4 (over y_lo, core).
Axes of the slice: x: 4, y: 4 (y_hi: 2, y_lo: 2; y = y_hi * 2 + y_lo), z: 8, core: 2. Of those that a mesh axis runs over, the one named last changes fastest.
Arguments:
- given_load: float32 [3, 512, 64, 256], P(None, 'sector', 'band'), may hold values from -20 to 20, as said below
- displacement: float32 [3, 512, 64, 256], P(None, 'sector', 'band'), may hold values from -3 to 3
- mass_coef: float32 [512, 64, 256], P('sector', 'band'), may hold values from 0.05 to 0.5
- stiffness: float32 [512, 64, 256], P('sector', 'band'), may hold values from 0.5 to 2
- bearing_node: int32 [1024], P(('sector', 'band')), may hold values from 0 to 2047
- stick_state: int32 [1024], P(('sector', 'band')), may hold values 0 or 1
- slip_prev: float32 [2, 1024], P(None, ('sector', 'band')), may hold values from -3 to 3
- bearing_old: float32 [2, 1024], P(None, ('sector', 'band')), may hold values from -3 to 3
- bearing_weight: float32 [1024], P(('sector', 'band')), may hold values from 4 to 16
Outputs:
- increment: float32 [3, 512, 64, 256], P(None, 'sector', 'band')
- cg_residual: float32 [3, 512, 64, 256], P(None, 'sector', 'band')
- bearing_force: float32 [3, 1024], P(None, ('sector', 'band'))
Inputs may be any that keep to these rules, and one draw needn't show every extreme that they name: `bearing_node`: each index names a node of the raft-base layer within the bearing's own sector; several bearings may share a node. `given_load`: loads of order one to a few tens.
All inputs are finite; a program needn't handle non-finite values. No bound on the sum of `stick_state` on one device may be relied on, other than what follows from the above.
Results may differ from a plain program's by a relative error of at most 0.00021.
Values sent between devices are 32-bit elements; how exact they have to be, the bound alone decides.
A program may use at most 64 MiB of HBM per device.

v0:
```python
import jax
import jax.numpy as jnp
from jax import lax
from jax.sharding import PartitionSpec as P

ITERS = 4


K_STICK = 4.0
K_VERT = 8.0
MU_FAST = 0.15
MU_SLOW = 0.04
RATE_GAIN = 2.0
RATE_DECAY = 2.0
V_FLOOR = 0.05
COMPONENT_SCALE = (1.0, 1.0, 2.0)
HIGHEST = lax.Precision.HIGHEST


def padded(x, sides, width, wrap):
    for axis, dim in sides:
        size, length = (lax.axis_size(axis), x.shape[dim])
        up = [(i, (i + 1) % size) for i in range(size if wrap else size - 1)]
        down = [(j, i) for i, j in up]
        last = lax.slice_in_dim(x, length - width, length, axis=dim)
        leading = lax.slice_in_dim(x, 0, width, axis=dim)
        before = lax.ppermute(last, axis, up)
        after = lax.ppermute(leading, axis, down)
        x = jnp.concatenate([before, x, after], axis=dim)
    return x


def from_root(value, axis, source):
    kept = jnp.where(lax.axis_index(axis) == source, value, 0).astype(value.dtype)
    return lax.psum(kept, axis)


def face_conductance(left, right):
    return 2.0 * left * right / (left + right)


def local_conductances(stiffness):
    cycle_padded = padded(stiffness, (("sector", 0),), 1, True)
    cond_sector = face_conductance(cycle_padded[:-1], cycle_padded[1:])
    height_padded = padded(stiffness, (("band", 1),), 1, False)
    cond_height = face_conductance(height_padded[:, :-1], height_padded[:, 1:])
    cond_radial = face_conductance(stiffness[:, :, :-1], stiffness[:, :, 1:])
    return (cond_sector, cond_height, cond_radial)


def field_faces(field):
    cycle_padded = padded(field, (("sector", 1),), 1, True)
    height_padded = padded(field, (("band", 2),), 1, False)
    return (cycle_padded, height_padded)


def operate(field, mass_coef, conds, bottom_diag):
    cond_sector, cond_height, cond_radial = conds
    scales = jnp.array(COMPONENT_SCALE, jnp.float32)[:, None, None, None]
    cycle_padded, height_padded = field_faces(field)
    flux_sector = cond_sector[None] * (cycle_padded[:, 1:] - cycle_padded[:, :-1])
    total = -(flux_sector[:, 1:] - flux_sector[:, :-1])
    flux_height = cond_height[None] * (height_padded[:, :, 1:] - height_padded[:, :, :-1])
    total = total - (flux_height[:, :, 1:] - flux_height[:, :, :-1])
    flux_radial = cond_radial[None] * (field[..., 1:] - field[..., :-1])
    flux_radial = jnp.pad(flux_radial, ((0, 0), (0, 0), (0, 0), (1, 1)))
    total = total - (flux_radial[..., 1:] - flux_radial[..., :-1])
    layers = field.shape[2]
    diag_full = jnp.pad(bottom_diag[:, :, None, :], ((0, 0), (0, 0), (0, layers - 1), (0, 0)))
    return mass_coef[None] * field + scales * total + diag_full * field


def bearing_law(at_node, stick_state, slip_prev, bearing_old, bearing_weight):
    moved = at_node[:2]
    trial = K_STICK * (moved - slip_prev)
    slip_rate = RATE_GAIN * (moved - bearing_old)
    slip_speed = jnp.sqrt(
        slip_rate[0] * slip_rate[0] + slip_rate[1] * slip_rate[1] + V_FLOOR * V_FLOOR
    )
    friction = MU_FAST - (MU_FAST - MU_SLOW) * jnp.exp(-RATE_DECAY * slip_speed)
    capacity = friction * bearing_weight
    magnitude = jnp.sqrt(trial[0] * trial[0] + trial[1] * trial[1])
    sliding = capacity[None] * trial / jnp.maximum(magnitude, capacity)[None]
    sticking = stick_state[None] == 1
    horizontal = jnp.where(sticking, trial, sliding)
    vertical = K_VERT * at_node[2]
    force = jnp.concatenate([horizontal, vertical[None]], axis=0)
    stick_k = jnp.where(stick_state == 1, K_STICK, 0.0).astype(jnp.float32)
    stiff = jnp.stack([stick_k, stick_k, jnp.full_like(stick_k, K_VERT)], axis=0)
    return (force, stiff)


def node_selector(nodes, count):
    positions = jnp.arange(count, dtype=jnp.int32)
    return (nodes[:, None] == positions[None, :]).astype(jnp.float32)


def bearings_on_row(raft_flat, nodes, stick_state, slip_prev, bearing_old, bearing_weight):
    selector = node_selector(nodes, raft_flat.shape[1])
    at_node = jnp.dot(raft_flat, selector.T, precision=HIGHEST, preferred_element_type=jnp.float32)
    force, stiff = bearing_law(at_node, stick_state, slip_prev, bearing_old, bearing_weight)
    loads = jnp.dot(force, selector, precision=HIGHEST, preferred_element_type=jnp.float32)
    bottom = jnp.dot(stiff, selector, precision=HIGHEST, preferred_element_type=jnp.float32)
    return (force, loads, bottom)


def residual_squares(residual):
    return lax.psum(jnp.sum(residual * residual), ("sector", "band"))


def per_device(
    given_load,
    displacement,
    mass_coef,
    stiffness,
    bearing_node,
    stick_state,
    slip_prev,
    bearing_old,
    bearing_weight,
):
    comps, rows_here, layers, radial = displacement.shape
    conds = local_conductances(stiffness)
    band_index = lax.axis_index("band")
    on_raft = (band_index == 0).astype(jnp.float32)
    raft_local = displacement[:, :, 0, :].reshape(comps, rows_here * radial)
    raft_flat = from_root(raft_local, "band", 0)
    own_force, loads, bottom = bearings_on_row(
        raft_flat, bearing_node, stick_state, slip_prev, bearing_old, bearing_weight
    )
    loads, bottom = lax.psum((loads, bottom), "band")
    loads = (loads * on_raft).reshape(comps, rows_here, radial)
    bottom = (bottom * on_raft).reshape(comps, rows_here, radial)
    zero_diag = jnp.zeros_like(bottom)
    load_full = jnp.pad(loads[:, :, None, :], ((0, 0), (0, 0), (0, layers - 1), (0, 0)))
    newton_rhs = given_load - operate(displacement, mass_coef, conds, zero_diag) - load_full
    increment = jnp.zeros_like(newton_rhs)
    residual = newton_rhs
    direction = newton_rhs
    norm_now = residual_squares(residual)
    for iteration in range(ITERS):
        image = operate(direction, mass_coef, conds, bottom)
        alpha = norm_now / lax.psum(jnp.sum(direction * image), ("sector", "band"))
        increment = increment + alpha * direction
        residual = residual - alpha * image
        norm_next = residual_squares(residual)
        direction = residual + norm_next / norm_now * direction
        norm_now = norm_next
    return (increment, residual, own_force)


def solution(mesh):
    return jax.shard_map(
        per_device,
        mesh=mesh,
        in_specs=(
            P(None, "sector", "band", None),
            P(None, "sector", "band", None),
            P("sector", "band", None),
            P("sector", "band", None),
            P(("sector", "band")),
            P(("sector", "band")),
            P(None, ("sector", "band")),
            P(None, ("sector", "band")),
            P(("sector", "band")),
        ),
        out_specs=(
            P(None, "sector", "band", None),
            P(None, "sector", "band", None),
            P(None, ("sector", "band")),
        ),
        check_vma=False,
    )
```

profile of v0, /device:TPU:1, one launch (start us, length us, event | category | flops | bytes accessed | tf_op | source)
XLA Modules:
  0.0 663.4 jit_solution(800022106437176982)
XLA Ops:
  1.6 4.6 collective-permute-start.4
  8.8 10.1 %collective-permute-start.1 = (f32[1,16,256]{2,1,0:T(8,128)S(1)}, f32[1,16,256]{2,1,0:T(8,128)S(1)}, u32[]{:S(2)}, u32[]{:S(2)}) collective-permute-start(f32[1,16,256]{2,1,0:T(8,128)S(1)} %get-tuple-element.43), channel_id=1, source_target_pairs={{4,0},{8,4},{12,8},{16,12},{20,16},{24,20},{28,24},{32,28},{36,32}... | collective-permute-start | bytes 49160 | tf_op jit(solution)/shard_map/ppermute | solution.py:28
  22.2 10.3 %psum.77 = f32[3,2048]{1,0:T(4,128)S(1)} all-reduce(f32[3,2048]{1,0:T(4,128)S(1)} %bitcast.11), channel_id=1, replica_groups=mesh['sector'=64,'band'=4] {'band'}, use_global_device_ids=true, to_apply=%region_0.1 | all-reduce | flops 6144 | bytes 49152 | tf_op jit(solution)/shard_map/psum | solution.py:35
  35.0 11.9 %all-reduce.8 = (f32[3,2048]{1,0:T(4,128)S(1)}, f32[3,2048]{1,0:T(4,128)S(1)}) all-reduce(f32[3,2048]{1,0:T(4,128)S(1)} %fusion.52, f32[3,2048]{1,0:T(4,128)S(1)} %fusion.51), channel_id=1, replica_groups=mesh['sector'=64,'band'=4] {'band'}, use_global_device_ids=true, to_apply=%region_1.2 | all-reduce | flops 12288 | bytes 98304 | tf_op jit(solution)/shard_map/psum | solution.py:131
  47.3 2.7 collective-permute-start.7
  50.2 7.9 %collective-permute-start.2 = (f32[3,1,16,256]{3,2,1,0:T(8,128)S(1)}, f32[3,1,16,256]{3,2,1,0:T(8,128)S(1)}, u32[]{:S(2)}, u32[]{:S(2)}) collective-permute-start(f32[3,1,16,256]{3,2,1,0:T(8,128)S(1)} %get-tuple-element.42), channel_id=1, source_target_pairs={{4,0},{8,4},{12,8},{16,12},{20,16},{24,20},{28,24},{32,28},{36,32}... | collective-permute-start | bytes 147464 | tf_op jit(solution)/shard_map/ppermute | solution.py:28
  62.6 2.3 collective-permute-start.10
  65.0 7.9 %collective-permute-start.8 = (f32[3,1,16,256]{3,2,1,0:T(8,128)S(1)}, f32[3,1,16,256]{3,2,1,0:T(8,128)S(1)}, u32[]{:S(2)}, u32[]{:S(2)}) collective-permute-start(f32[3,1,16,256]{3,2,1,0:T(8,128)S(1)} %get-tuple-element.35), channel_id=1, source_target_pairs={{4,0},{8,4},{12,8},{16,12},{20,16},{24,20},{28,24},{32,28},{36,32}... | collective-permute-start | bytes 147464 | tf_op jit(solution)/shard_map/ppermute | solution.py:28
  75.3 76.8 %all-reduce.7 = (f32[]{:T(128)}, f32[]{:T(128)}) all-reduce(f32[]{:T(128)} %get-tuple-element.4, f32[]{:T(128)} %get-tuple-element.3), channel_id=1, replica_groups=mesh['sector'=64,'band'=4] {'sector','band'}, use_global_device_ids=true, to_apply=%region_3.4 | all-reduce | flops 2 | bytes 16 | tf_op jit(solution)/shard_map/psum | solution.py:108
  154.2 73.3 %psum.82 = f32[]{:T(128)} all-reduce(f32[]{:T(128)} %multiply_reduce_fusion.5), channel_id=1, replica_groups=mesh['sector'=64,'band'=4] {'sector','band'}, use_global_device_ids=true, to_apply=%region_8.9 | all-reduce | flops 1 | bytes 8 | tf_op jit(solution)/shard_map/psum | solution.py:108
  229.2 3.4 collective-permute-start.15
  234.5 2.5 collective-permute-start.13
  237.0 4.8 collective-permute-start.12
  244.3 77.3 %psum.83 = f32[]{:T(128)} all-reduce(f32[]{:T(128)} %get-tuple-element.17), channel_id=1, replica_groups=mesh['sector'=64,'band'=4] {'sector','band'}, use_global_device_ids=true, to_apply=%region_10.11 | all-reduce | flops 1 | bytes 8 | tf_op jit(solution)/shard_map/psum | solution.py:143
  323.6 73.4 %psum.84 = f32[]{:T(128)} all-reduce(f32[]{:T(128)} %get-tuple-element.15), channel_id=1, replica_groups=mesh['sector'=64,'band'=4] {'sector','band'}, use_global_device_ids=true, to_apply=%region_12.13 | all-reduce | flops 1 | bytes 8 | tf_op jit(solution)/shard_map/psum | solution.py:108
  398.7 3.6 collective-permute-start.19
  404.2 2.5 collective-permute-start.17
  406.7 4.8 collective-permute-start.16
  414.0 77.3 %psum.85 = f32[]{:T(128)} all-reduce(f32[]{:T(128)} %get-tuple-element.13), channel_id=1, replica_groups=mesh['sector'=64,'band'=4] {'sector','band'}, use_global_device_ids=true, to_apply=%region_14.15 | all-reduce | flops 1 | bytes 8 | tf_op jit(solution)/shard_map/psum | solution.py:143
  493.3 73.4 %psum.86 = f32[]{:T(128)} all-reduce(f32[]{:T(128)} %get-tuple-element.11), channel_id=1, replica_groups=mesh['sector'=64,'band'=4] {'sector','band'}, use_global_device_ids=true, to_apply=%region_16.17 | all-reduce | flops 1 | bytes 8 | tf_op jit(solution)/shard_map/psum | solution.py:108
  568.3 3.6 collective-permute-start.23
  573.9 2.5 collective-permute-start.21
  576.4 4.8 collective-permute-start.20
  583.6 77.3 %psum.87 = f32[]{:T(128)} all-reduce(f32[]{:T(128)} %get-tuple-element.9), channel_id=1, replica_groups=mesh['sector'=64,'band'=4] {'sector','band'}, use_global_device_ids=true, to_apply=%region_18.19 | all-reduce | flops 1 | bytes 8 | tf_op jit(solution)/shard_map/psum | solution.py:143
  (118 shorter events, 33.8 us)
Async XLA Ops:
  1.6 56.6 %collective-permute-start.4 = (f32[8,1,256]{2,1,0:T(1,128)S(1)}, f32[8,1,256]{2,1,0:T(1,128)S(1)}, u32[]{:S(2)}, u32[]{:S(2)}) collective-permute-start(f32[8,1,256]{2,1,0:T(1,128)S(1)} %get-tuple-element.48), channel_id=1, source_target_pairs={{0,1},{1,2},{2,3},{4,5},{5,6},{6,7},{8,9},{9,10},{10,11},{12,13},{... | collective-permute-start | bytes 24584 | tf_op jit(solution)/shard_map/ppermute | solution.py:27
  6.2 44.0 %collective-permute-start.5 = (f32[8,1,256]{2,1,0:T(1,128)S(1)}, f32[8,1,256]{2,1,0:T(1,128)S(1)}, u32[]{:S(2)}, u32[]{:S(2)}) collective-permute-start(f32[8,1,256]{2,1,0:T(1,128)S(1)} %get-tuple-element.49), channel_id=1, source_target_pairs={{1,0},{2,1},{3,2},{5,4},{6,5},{7,6},{9,8},{10,9},{11,10},{13,12},{... | collective-permute-start | bytes 24584 | tf_op jit(solution)/shard_map/ppermute | solution.py:28
  8.8 41.2 %collective-permute-start.1 = (f32[1,16,256]{2,1,0:T(8,128)S(1)}, f32[1,16,256]{2,1,0:T(8,128)S(1)}, u32[]{:S(2)}, u32[]{:S(2)}) collective-permute-start(f32[1,16,256]{2,1,0:T(8,128)S(1)} %get-tuple-element.43), channel_id=1, source_target_pairs={{4,0},{8,4},{12,8},{16,12},{20,16},{24,20},{28,24},{32,28},{36,32}... | collective-permute-start | bytes 49160 | tf_op jit(solution)/shard_map/ppermute | solution.py:28
  18.9 28.3 %collective-permute-start = (f32[1,16,256]{2,1,0:T(8,128)S(1)}, f32[1,16,256]{2,1,0:T(8,128)S(1)}, u32[]{:S(2)}, u32[]{:S(2)}) collective-permute-start(f32[1,16,256]{2,1,0:T(8,128)S(1)} %get-tuple-element.44), channel_id=1, source_target_pairs={{0,4},{4,8},{8,12},{12,16},{16,20},{20,24},{24,28},{28,32},{32,36}... | collective-permute-start | bytes 49160 | tf_op jit(solution)/shard_map/ppermute | solution.py:27
  20.1 38.2 %collective-permute-start.6 = (f32[3,8,1,256]{3,2,1,0:T(1,128)S(1)}, f32[3,8,1,256]{3,2,1,0:T(1,128)S(1)}, u32[]{:S(2)}, u32[]{:S(2)}) collective-permute-start(f32[3,8,1,256]{3,2,1,0:T(1,128)S(1)} %get-tuple-element.39), channel_id=1, source_target_pairs={{1,0},{2,1},{3,2},{5,4},{6,5},{7,6},{9,8},{10,9},{11,10},{13,12},{... | collective-permute-start | bytes 73736 | tf_op jit(solution)/shard_map/ppermute | solution.py:28
  47.3 11.0 %collective-permute-start.7 = (f32[3,8,1,256]{3,2,1,0:T(1,128)S(1)}, f32[3,8,1,256]{3,2,1,0:T(1,128)S(1)}, u32[]{:S(2)}, u32[]{:S(2)}) collective-permute-start(f32[3,8,1,256]{3,2,1,0:T(1,128)S(1)} %get-tuple-element.40), channel_id=1, source_target_pairs={{0,1},{1,2},{2,3},{4,5},{5,6},{6,7},{8,9},{9,10},{10,11},{12,13},{... | collective-permute-start | bytes 73736 | tf_op jit(solution)/shard_map/ppermute | solution.py:27
  50.0 9.9 %collective-permute-start.3 = (f32[3,1,16,256]{3,2,1,0:T(8,128)S(1)}, f32[3,1,16,256]{3,2,1,0:T(8,128)S(1)}, u32[]{:S(2)}, u32[]{:S(2)}) collective-permute-start(f32[3,1,16,256]{3,2,1,0:T(8,128)S(1)} %get-tuple-element.41), channel_id=1, source_target_pairs={{0,4},{4,8},{8,12},{12,16},{16,20},{20,24},{24,28},{28,32},{32,36}... | collective-permute-start | bytes 147464 | tf_op jit(solution)/shard_map/ppermute | solution.py:27
  50.2 9.7 %collective-permute-start.2 = (f32[3,1,16,256]{3,2,1,0:T(8,128)S(1)}, f32[3,1,16,256]{3,2,1,0:T(8,128)S(1)}, u32[]{:S(2)}, u32[]{:S(2)}) collective-permute-start(f32[3,1,16,256]{3,2,1,0:T(8,128)S(1)} %get-tuple-element.42), channel_id=1, source_target_pairs={{4,0},{8,4},{12,8},{16,12},{20,16},{24,20},{28,24},{32,28},{36,32}... | collective-permute-start | bytes 147464 | tf_op jit(solution)/shard_map/ppermute | solution.py:28
  60.6 12.3 %collective-permute-start.11 = (f32[3,8,1,256]{3,2,1,0:T(1,128)S(1)}, f32[3,8,1,256]{3,2,1,0:T(1,128)S(1)}, u32[]{:S(2)}, u32[]{:S(2)}) collective-permute-start(f32[3,8,1,256]{3,2,1,0:T(1,128)S(1)} %get-tuple-element.36), channel_id=1, source_target_pairs={{0,1},{1,2},{2,3},{4,5},{5,6},{6,7},{8,9},{9,10},{10,11},{12,13},{... | collective-permute-start | bytes 73736 | tf_op jit(solution)/shard_map/ppermute | solution.py:27
  62.6 10.3 %collective-permute-start.10 = (f32[3,8,1,256]{3,2,1,0:T(1,128)S(1)}, f32[3,8,1,256]{3,2,1,0:T(1,128)S(1)}, u32[]{:S(2)}, u32[]{:S(2)}) collective-permute-start(f32[3,8,1,256]{3,2,1,0:T(1,128)S(1)} %get-tuple-element.37), channel_id=1, source_target_pairs={{1,0},{2,1},{3,2},{5,4},{6,5},{7,6},{9,8},{10,9},{11,10},{13,12},{... | collective-permute-start | bytes 73736 | tf_op jit(solution)/shard_map/ppermute | solution.py:28
  64.9 9.4 %collective-permute-start.9 = (f32[3,1,16,256]{3,2,1,0:T(8,128)S(1)}, f32[3,1,16,256]{3,2,1,0:T(8,128)S(1)}, u32[]{:S(2)}, u32[]{:S(2)}) collective-permute-start(f32[3,1,16,256]{3,2,1,0:T(8,128)S(1)} %get-tuple-element.34), channel_id=1, source_target_pairs={{0,4},{4,8},{8,12},{12,16},{16,20},{20,24},{24,28},{28,32},{32,36}... | collective-permute-start | bytes 147464 | tf_op jit(solution)/shard_map/ppermute | solution.py:27
  65.0 9.3 %collective-permute-start.8 = (f32[3,1,16,256]{3,2,1,0:T(8,128)S(1)}, f32[3,1,16,256]{3,2,1,0:T(8,128)S(1)}, u32[]{:S(2)}, u32[]{:S(2)}) collective-permute-start(f32[3,1,16,256]{3,2,1,0:T(8,128)S(1)} %get-tuple-element.35), channel_id=1, source_target_pairs={{4,0},{8,4},{12,8},{16,12},{20,16},{24,20},{28,24},{32,28},{36,32}... | collective-permute-start | bytes 147464 | tf_op jit(solution)/shard_map/ppermute | solution.py:28
  229.2 12.6 %collective-permute-start.15 = (f32[3,8,1,256]{3,2,1,0:T(1,128)S(1)}, f32[3,8,1,256]{3,2,1,0:T(1,128)S(1)}, u32[]{:S(2)}, u32[]{:S(2)}) collective-permute-start(f32[3,8,1,256]{3,2,1,0:T(1,128)S(1)} %get-tuple-element.32), channel_id=1, source_target_pairs={{0,1},{1,2},{2,3},{4,5},{5,6},{6,7},{8,9},{9,10},{10,11},{12,13},{... | collective-permute-start | bytes 73736 | tf_op jit(solution)/shard_map/ppermute | solution.py:27
  232.6 9.2 %collective-permute-start.14 = (f32[3,8,1,256]{3,2,1,0:T(1,128)S(1)}, f32[3,8,1,256]{3,2,1,0:T(1,128)S(1)}, u32[]{:S(2)}, u32[]{:S(2)}) collective-permute-start(f32[3,8,1,256]{3,2,1,0:T(1,128)S(1)} %get-tuple-element.33), channel_id=1, source_target_pairs={{1,0},{2,1},{3,2},{5,4},{6,5},{7,6},{9,8},{10,9},{11,10},{13,12},{... | collective-permute-start | bytes 73736 | tf_op jit(solution)/shard_map/ppermute | solution.py:28
  234.5 8.7 %collective-permute-start.13 = (f32[3,1,16,256]{3,2,1,0:T(8,128)S(1)}, f32[3,1,16,256]{3,2,1,0:T(8,128)S(1)}, u32[]{:S(2)}, u32[]{:S(2)}) collective-permute-start(f32[3,1,16,256]{3,2,1,0:T(8,128)S(1)} %get-tuple-element.30), channel_id=1, source_target_pairs={{0,4},{4,8},{8,12},{12,16},{16,20},{20,24},{24,28},{28,32},{32,36}... | collective-permute-start | bytes 147464 | tf_op jit(solution)/shard_map/ppermute | solution.py:27
  237.0 6.3 collective-permute-start.12
  398.7 12.8 %collective-permute-start.19 = (f32[3,8,1,256]{3,2,1,0:T(1,128)S(1)}, f32[3,8,1,256]{3,2,1,0:T(1,128)S(1)}, u32[]{:S(2)}, u32[]{:S(2)}) collective-permute-start(f32[3,8,1,256]{3,2,1,0:T(1,128)S(1)} %get-tuple-element.28), channel_id=1, source_target_pairs={{0,1},{1,2},{2,3},{4,5},{5,6},{6,7},{8,9},{9,10},{10,11},{12,13},{... | collective-permute-start | bytes 73736 | tf_op jit(solution)/shard_map/ppermute | solution.py:27
  402.3 9.2 %collective-permute-start.18 = (f32[3,8,1,256]{3,2,1,0:T(1,128)S(1)}, f32[3,8,1,256]{3,2,1,0:T(1,128)S(1)}, u32[]{:S(2)}, u32[]{:S(2)}) collective-permute-start(f32[3,8,1,256]{3,2,1,0:T(1,128)S(1)} %get-tuple-element.29), channel_id=1, source_target_pairs={{1,0},{2,1},{3,2},{5,4},{6,5},{7,6},{9,8},{10,9},{11,10},{13,12},{... | collective-permute-start | bytes 73736 | tf_op jit(solution)/shard_map/ppermute | solution.py:28
  404.2 8.7 %collective-permute-start.17 = (f32[3,1,16,256]{3,2,1,0:T(8,128)S(1)}, f32[3,1,16,256]{3,2,1,0:T(8,128)S(1)}, u32[]{:S(2)}, u32[]{:S(2)}) collective-permute-start(f32[3,1,16,256]{3,2,1,0:T(8,128)S(1)} %get-tuple-element.26), channel_id=1, source_target_pairs={{0,4},{4,8},{8,12},{12,16},{16,20},{20,24},{24,28},{28,32},{32,36}... | collective-permute-start | bytes 147464 | tf_op jit(solution)/shard_map/ppermute | solution.py:27
  406.7 6.3 collective-permute-start.16
  568.3 12.8 %collective-permute-start.23 = (f32[3,8,1,256]{3,2,1,0:T(1,128)S(1)}, f32[3,8,1,256]{3,2,1,0:T(1,128)S(1)}, u32[]{:S(2)}, u32[]{:S(2)}) collective-permute-start(f32[3,8,1,256]{3,2,1,0:T(1,128)S(1)} %get-tuple-element.24), channel_id=1, source_target_pairs={{0,1},{1,2},{2,3},{4,5},{5,6},{6,7},{8,9},{9,10},{10,11},{12,13},{... | collective-permute-start | bytes 73736 | tf_op jit(solution)/shard_map/ppermute | solution.py:27
  571.9 9.2 %collective-permute-start.22 = (f32[3,8,1,256]{3,2,1,0:T(1,128)S(1)}, f32[3,8,1,256]{3,2,1,0:T(1,128)S(1)}, u32[]{:S(2)}, u32[]{:S(2)}) collective-permute-start(f32[3,8,1,256]{3,2,1,0:T(1,128)S(1)} %get-tuple-element.25), channel_id=1, source_target_pairs={{1,0},{2,1},{3,2},{5,4},{6,5},{7,6},{9,8},{10,9},{11,10},{13,12},{... | collective-permute-start | bytes 73736 | tf_op jit(solution)/shard_map/ppermute | solution.py:28
  573.9 8.7 %collective-permute-start.21 = (f32[3,1,16,256]{3,2,1,0:T(8,128)S(1)}, f32[3,1,16,256]{3,2,1,0:T(8,128)S(1)}, u32[]{:S(2)}, u32[]{:S(2)}) collective-permute-start(f32[3,1,16,256]{3,2,1,0:T(8,128)S(1)} %get-tuple-element.22), channel_id=1, source_target_pairs={{0,4},{4,8},{8,12},{12,16},{16,20},{20,24},{24,28},{28,32},{32,36}... | collective-permute-start | bytes 147464 | tf_op jit(solution)/shard_map/ppermute | solution.py:27
  576.4 6.3 collective-permute-start.20
  (11 other events, 66.1 us)
where the time goes:
time: 665 us; the launch traced here: 663 us
  blocking collectives  551 us (83%)
  starting transfers between devices  79.7 us (12%)
  other arithmetic  10.7 us (2%)
  between operations  10.6 us (2%)
  waiting for transfers between devices  6.91 us (1%)
    psum x4, blocking collectives, residual_squares(): return lax.psum(jnp.sum(residual * residual), ('sector', 'band'))  297 us
    psum x3, blocking collectives, per_device(): alpha = norm_now / lax.psum(jnp.sum(direction * image), ('sector', 'band'))  232 us
    ppermute x12, starting transfers between devices, padded(): after = lax.ppermute(leading, axis, down)  52.2 us
    ppermute x12, starting transfers between devices, padded(): before = lax.ppermute(last, axis, up)  27.5 us
  transfers between devices with their start and end apart: 24, of which 5 were waited for; matrix products, arithmetic and copies ran while one was open for 1% of the time, Pallas kernels for 0%

commit v1 on v0

v1 whole, which is shorter than its diff:
```python
import functools

import jax
import jax.numpy as jnp
from jax import lax
from jax.experimental import pallas as pl
from jax.experimental.pallas import tpu as pltpu
from jax.sharding import PartitionSpec as P

ITERS = 4
K_STICK = 4.0
K_VERT = 8.0
MU_FAST = 0.15
MU_SLOW = 0.04
RATE_GAIN = 2.0
RATE_DECAY = 2.0
V_FLOOR = 0.05
HIGHEST = lax.Precision.HIGHEST
MESH = pl.DeviceIdType.MESH

C = 14.0
E = 14.0
CA = 8
LAYERS = 16
NR = 256
DEPTH = 4
ROWS = CA + 2 * DEPTH
LEV = LAYERS + 2 * DEPTH
N_SECTOR = 64
N_BAND = 4
NX = 4
NZ = 8
PAIRS = [(0, 0), (0, 1), (1, 1), (0, 2), (1, 2), (2, 2), (0, 3), (1, 3), (2, 3), (3, 3), (0, 4), (1, 4), (2, 4), (3, 4)]


def coefficients(gram):
    def apply(d):
        q = [None] * 5

        def add(k, v):
            q[k] = v if q[k] is None else q[k] + v

        for j, dj in enumerate(d):
            add(j, C * dj)
            if j == 0:
                add(1, E * dj)
            else:
                add(j + 1, (E / 2) * dj)
                add(j - 1, (E / 2) * dj)
        return [v for v in q if v is not None]

    def inner(a, b):
        total = None
        for i, ai in enumerate(a):
            for j, bj in enumerate(b):
                term = ai * bj * gram(min(i, j), max(i, j))
                total = term if total is None else total + term
        return total

    def padded_add(a, b, scale):
        out = []
        for i in range(max(len(a), len(b))):
            if i >= len(a):
                out.append(scale * b[i])
            elif i >= len(b):
                out.append(a[i])
            else:
                out.append(a[i] + scale * b[i])
        return out

    one = jnp.ones_like(gram(0, 0))
    r, d, x = [one], [one], []
    rr = gram(0, 0)
    for k in range(ITERS):
        q = apply(d)
        alpha = rr / inner(d, q)
        x = padded_add(x, d, alpha)
        r = padded_add(r, q, -alpha)
        if k < ITERS - 1:
            new = inner(r, r)
            d = padded_add(r, d, new / rr)
            rr = new
    return x, r


def kernel(
    load_hbm,
    disp_hbm,
    mass_hbm,
    stiff_hbm,
    node_ref,
    stick_ref,
    slip_ref,
    old_ref,
    weight_ref,
    inc_ref,
    res_ref,
    force_ref,
    st,
    me,
    u,
    p,
    k_row,
    k_up,
    k_dn,
    k_in,
    k_out,
    diag,
    bdiag,
    loads,
    pack,
    packs,
    forces,
    force_in,
    gtile,
    red_a,
    red_b,
    red_c,
    load_sem,
    send_sem,
    recv_sem,
    pack_send,
    pack_recv,
    force_send,
    force_recv,
    ra_send,
    ra_recv,
    rb_send,
    rb_recv,
    rc_send,
    rc_recv,
):
    s = lax.axis_index("sector")
    b = lax.axis_index("band")
    z, x, yh = s // 8, lax.rem(s // 2, 4), lax.rem(s, 2)
    s_dn, s_up = lax.rem(s + N_SECTOR - 1, N_SECTOR), lax.rem(s + 1, N_SECTOR)
    low, high = b == 0, b == N_BAND - 1

    group_a = []
    for da in range(2):
        for db in range(4):
            if (da, db) != (0, 0):
                group_a.append(((s // 2) * 2 + lax.rem(yh + da, 2), lax.rem(b + db, 4)))
    group_b = [((z * 4 + lax.rem(x + i, 4)) * 2 + yh, b) for i in range(1, NX)]
    group_c = [((lax.rem(z + i, 8) * 4 + x) * 2 + yh, b) for i in range(1, NZ)]

    local = [
        pltpu.make_async_copy(stiff_hbm, st.at[0:CA, 0:LAYERS, :], load_sem.at[0]),
        pltpu.make_async_copy(disp_hbm, u.at[:, 0:CA, 0:LAYERS, :], load_sem.at[1]),
        pltpu.make_async_copy(mass_hbm, me.at[0:CA, 0:LAYERS, :], load_sem.at[2]),
        pltpu.make_async_copy(load_hbm, p.at[0, :, 0:CA, 0:LAYERS, :], load_sem.at[3]),
    ]
    for copy in local:
        copy.start()

    barrier = pltpu.get_barrier_semaphore()
    everyone = [(s_dn, b), (s_up, b)] + group_a + group_b + group_c
    for target in everyone:
        pl.semaphore_signal(barrier, inc=1, device_id=target, device_id_type=MESH)

    pack[...] = jnp.zeros_like(pack)
    pack[0:1, 0:4] = node_ref[...].astype(jnp.float32)
    pack[1:2, 0:4] = stick_ref[...].astype(jnp.float32)
    pack[2:4, 0:4] = slip_ref[...]
    pack[4:6, 0:4] = old_ref[...]
    pack[6:7, 0:4] = weight_ref[...]

    @pl.when(low)
    def _():
        st[:, LEV - DEPTH : LEV, :] = jnp.zeros((ROWS, DEPTH, NR), jnp.float32)
        me[:, LEV - DEPTH : LEV, :] = jnp.zeros((ROWS, DEPTH, NR), jnp.float32)
        u[:, 0:CA, LEV - 1 : LEV, :] = jnp.zeros((3, CA, 1, NR), jnp.float32)
        p[0, :, :, LEV - DEPTH : LEV, :] = jnp.zeros((3, ROWS, DEPTH, NR), jnp.float32)

    @pl.when(high)
    def _():
        st[:, LAYERS : LAYERS + DEPTH, :] = jnp.zeros((ROWS, DEPTH, NR), jnp.float32)
        me[:, LAYERS : LAYERS + DEPTH, :] = jnp.zeros((ROWS, DEPTH, NR), jnp.float32)
        u[:, 0:CA, LAYERS : LAYERS + 1, :] = jnp.zeros((3, CA, 1, NR), jnp.float32)
        p[0, :, :, LAYERS : LAYERS + DEPTH, :] = jnp.zeros((3, ROWS, DEPTH, NR), jnp.float32)

    def remote(i, src, dst, target):
        return pltpu.make_async_remote_copy(
            src_ref=src,
            dst_ref=dst,
            send_sem=send_sem.at[i],
            recv_sem=recv_sem.at[i],
            device_id=target,
            device_id_type=MESH,
        )

    own, rim = slice(0, CA), slice(CA, ROWS)
    first, last = slice(0, DEPTH), slice(CA - DEPTH, CA)
    after, before = slice(CA, CA + DEPTH), slice(CA + DEPTH, ROWS)
    lay = slice(0, LAYERS)
    bottom, top = slice(0, DEPTH), slice(LAYERS - DEPTH, LAYERS)
    above, below = slice(LAYERS, LAYERS + DEPTH), slice(LAYERS + DEPTH, LEV)

    b_dn, b_up = (s, lax.rem(b + N_BAND - 1, N_BAND)), (s, lax.rem(b + 1, N_BAND))
    t_dn, t_up = (s_dn, b), (s_up, b)

    u_down = remote(8, disp_hbm.at[:, :, 0:1, :], u.at[:, own, LAYERS : LAYERS + 1, :], b_dn)
    u_up = remote(9, disp_hbm.at[:, :, LAYERS - 1 : LAYERS, :], u.at[:, own, LEV - 1 : LEV, :], b_up)
    st_down = remote(6, stiff_hbm.at[:, bottom, :], st.at[own, above, :], b_dn)
    st_up = remote(7, stiff_hbm.at[:, top, :], st.at[own, below, :], b_up)
    me_down = remote(10, mass_hbm.at[:, bottom, :], me.at[own, above, :], b_dn)
    me_up = remote(11, mass_hbm.at[:, top, :], me.at[own, below, :], b_up)
    st_first = remote(0, stiff_hbm.at[first], st.at[after, lay, :], t_dn)
    st_last = remote(1, stiff_hbm.at[last], st.at[before, lay, :], t_up)
    me_first = remote(2, mass_hbm.at[first], me.at[after, lay, :], t_dn)
    me_last = remote(3, mass_hbm.at[last], me.at[before, lay, :], t_up)
    u_first = remote(4, disp_hbm.at[:, 0:1], u.at[:, CA : CA + 1, lay, :], t_dn)
    u_last = remote(5, disp_hbm.at[:, CA - 1 : CA], u.at[:, ROWS - 1 : ROWS, lay, :], t_up)
    st_rim_down = remote(12, st.at[rim, bottom, :], st.at[rim, above, :], b_dn)
    st_rim_up = remote(13, st.at[rim, top, :], st.at[rim, below, :], b_up)
    me_rim_down = remote(14, me.at[rim, bottom, :], me.at[rim, above, :], b_dn)
    me_rim_up = remote(15, me.at[rim, top, :], me.at[rim, below, :], b_up)
    bd_first = remote(16, bdiag.at[:, first, :], bdiag.at[:, after, :], t_dn)
    bd_last = remote(17, bdiag.at[:, last, :], bdiag.at[:, before, :], t_up)
    p_first = remote(18, p.at[0, :, first, lay, :], p.at[0, :, after, lay, :], t_dn)
    p_last = remote(19, p.at[0, :, last, lay, :], p.at[0, :, before, lay, :], t_up)
    p_down = remote(20, p.at[0, :, :, bottom, :], p.at[0, :, :, above, :], b_dn)
    p_up = remote(21, p.at[0, :, :, top, :], p.at[0, :, :, below, :], b_up)

    def pack_copy(slot):
        return pltpu.make_async_remote_copy(
            src_ref=pack,
            dst_ref=packs.at[slot],
            send_sem=pack_send.at[slot],
            recv_sem=pack_recv.at[slot],
            device_id=(s, 0),
            device_id_type=MESH,
        )

    def force_copy(slot):
        return pltpu.make_async_remote_copy(
            src_ref=forces.at[slot],
            dst_ref=force_in,
            send_sem=force_send.at[slot],
            recv_sem=force_recv.at[0],
            device_id=(s, slot),
            device_id_type=MESH,
        )

    def downward(*copies):
        @pl.when(jnp.logical_not(low))
        def _():
            for copy in copies:
                copy.start()

    def upward(*copies):
        @pl.when(jnp.logical_not(high))
        def _():
            for copy in copies:
                copy.start()

    def from_bands(downs, ups):
        @pl.when(jnp.logical_not(high))
        def _():
            for copy in downs:
                copy.wait_recv()

        @pl.when(jnp.logical_not(low))
        def _():
            for copy in ups:
                copy.wait_recv()

    pl.semaphore_wait(barrier, len(everyone))

    for slot in range(1, N_BAND):

        @pl.when(b == slot)
        def _():
            pack_copy(slot).start()

    downward(u_down, st_down)
    upward(u_up, st_up)
    for copy in (st_first, st_last, u_first, u_last, me_first, me_last):
        copy.start()
    downward(me_down)
    upward(me_up)

    def face(a, c):
        return (4.0 / E) * a * c / jnp.maximum(a + c, 0.25)

    lane = lax.broadcasted_iota(jnp.int32, (LEV, NR), 1)

    def conductances_of(i):
        a = st[i]
        ku = face(a, pltpu.roll(a, LEV - 1, 0))
        ko = jnp.where(lane == NR - 1, 0.0, face(a, pltpu.roll(a, NR - 1, 1)))
        k_up[i] = ku
        k_dn[i] = pltpu.roll(ku, 1, 0)
        k_out[i] = ko
        k_in[i] = pltpu.roll(ko, 1, 1)

    local[0].wait()
    from_bands([u_down, st_down], [u_up, st_up])

    @pl.loop(0, CA)
    def _(i):
        conductances_of(i)

    @pl.loop(0, CA - 1)
    def _(i):
        k_row[i] = face(st[i], st[i + 1])

    local[1].wait()
    local[2].wait()
    local[3].wait()

    @pl.when(low)
    def _():
        packs[0] = pack[...]
        for slot in range(1, N_BAND):
            pack_copy(slot).wait_recv()
        t = packs[0]
        for slot in range(1, N_BAND):
            t = t + pltpu.roll(packs[slot], 4 * slot, 1)
        t = t[:, 0:128]
        node = t[0:1, :].astype(jnp.int32)
        stick = t[1:2, :] > 0.5
        row_of = node // NR
        col_of = lax.rem(node, NR)
        real = lax.broadcasted_iota(jnp.int32, (1, 128), 1) < 4 * N_BAND
        col_hot = jnp.where(
            jnp.logical_and(lax.broadcasted_iota(jnp.int32, (NR, 128), 0) == col_of, real), 1.0, 0.0
        ).astype(jnp.float32)
        row_hot = jnp.where(lax.broadcasted_iota(jnp.int32, (CA, 128), 0) == row_of, 1.0, 0.0).astype(jnp.float32)
        raft = jnp.concatenate([u[c, r, 0:1, :] for c in range(3) for r in range(CA)], axis=0)
        picked = jnp.dot(raft, col_hot, precision=HIGHEST, preferred_element_type=jnp.float32)
        at = [jnp.sum(picked[CA * c : CA * (c + 1)] * row_hot, axis=0, keepdims=True) for c in range(3)]
        trial = [K_STICK * (at[c] - t[2 + c : 3 + c]) for c in range(2)]
        rate = [RATE_GAIN * (at[c] - t[4 + c : 5 + c]) for c in range(2)]
        speed = jnp.sqrt(rate[0] * rate[0] + rate[1] * rate[1] + V_FLOOR * V_FLOOR)
        friction = MU_FAST - (MU_FAST - MU_SLOW) * jnp.exp(-RATE_DECAY * speed)
        capacity = friction * t[6:7]
        magnitude = jnp.sqrt(trial[0] * trial[0] + trial[1] * trial[1])
        largest = jnp.maximum(magnitude, capacity)
        largest = jnp.where(real, largest, 1.0)
        force = [jnp.where(stick, trial[c], capacity * trial[c] / largest) for c in range(2)]
        force = [jnp.where(real, f, 0.0) for f in force + [K_VERT * at[2]]]
        stick_k = jnp.where(jnp.logical_and(stick, real), K_STICK, 0.0)
        vert_k = jnp.where(real, K_VERT, 0.0)
        weights = jnp.concatenate([row_hot * v for v in force + [stick_k, vert_k]], axis=0)
        spread = lax.dot_general(
            weights, col_hot, (((1,), (1,)), ((), ())), precision=HIGHEST, preferred_element_type=jnp.float32
        )
        for c in range(3):
            loads[c] = spread[CA * c : CA * (c + 1)]
        bdiag[0, 0:CA] = spread[3 * CA : 4 * CA]
        bdiag[1, 0:CA] = spread[4 * CA : 5 * CA]
        tile = jnp.concatenate(force + [jnp.zeros((5, 128), jnp.float32)], axis=0)
        force_in[...] = tile
        for slot in range(1, N_BAND):
            forces[slot] = pltpu.roll(tile, 128 - 4 * slot, 1)
        for slot in range(1, N_BAND):
            force_copy(slot).start()

    @pl.when(jnp.logical_not(low))
    def _():
        loads[...] = jnp.zeros_like(loads)
        bdiag[:, 0:CA, :] = jnp.zeros((2, CA, NR), jnp.float32)

    bd_first.start()
    bd_last.start()

    gains = (1.0, 1.0, 2.0)
    layer = lax.broadcasted_iota(jnp.int32, (LAYERS, NR), 0)

    @pl.loop(0, CA)
    def _(i):
        up, dn = jnp.minimum(i + 1, CA - 1), jnp.maximum(i - 1, 0)
        on_up = jnp.where(i < CA - 1, 1.0, 0.0)
        kr_up = k_row[jnp.minimum(i, CA - 2), lay, :]
        kr_dn = k_row[dn, lay, :]
        ku, kd, ko, ki = k_up[i, lay, :], k_dn[i, lay, :], k_out[i, lay, :], k_in[i, lay, :]
        m = me[i, lay, :]
        for c in range(3):
            whole = u[c, i]
            v = whole[0:LAYERS]
            above_v = pltpu.roll(whole, LEV - 1, 0)[0:LAYERS]
            below_v = pltpu.roll(whole, 1, 0)[0:LAYERS]
            acc = ku * (above_v - v) + kd * (below_v - v)
            acc = acc + ko * (pltpu.roll(v, NR - 1, 1) - v) + ki * (pltpu.roll(v, 1, 1) - v)
            acc = acc + kr_up * (u[c, up, lay, :] - v) + kr_dn * (u[c, dn, lay, :] - v)
            rhs = p[0, c, i, lay, :] - m * v + (gains[c] * E / 2) * acc
            rhs = rhs - jnp.where(layer == 0, loads[c, pl.ds(i, 1), :], 0.0)
            p[0, c, i, lay, :] = rhs

    p_first.start()
    p_last.start()

    for copy in (st_first, st_last, me_first, me_last):
        copy.wait_recv()
    downward(st_rim_down, me_rim_down)
    upward(st_rim_up, me_rim_up)
    from_bands([me_down, st_rim_down, me_rim_down], [me_up, st_rim_up, me_rim_up])

    @pl.loop(CA, ROWS)
    def _(i):
        conductances_of(i)

    @pl.loop(CA - 1, ROWS)
    def _(i):
        k_row[i] = face(st[i], st[lax.rem(i + 1, ROWS)])

    for copy in (bd_first, bd_last):
        copy.wait_recv()
    lev = lax.broadcasted_iota(jnp.int32, (LEV, NR), 0)

    @pl.loop(0, ROWS)
    def _(i):
        near = k_up[i] + k_dn[i] + k_out[i] + k_in[i] + k_row[i] + k_row[lax.rem(i + ROWS - 1, ROWS)]
        base = (2.0 / E) * (me[i] - C)
        for h in range(2):
            extra = (2.0 / E) * bdiag[h, pl.ds(i, 1), :]
            diag[h, i] = base + (h + 1.0) * near + jnp.where(lev == 0, extra, 0.0)

    for copy in (p_first, p_last):
        copy.wait_send()
    for copy in (u_first, u_last, p_first, p_last):
        copy.wait_recv()
    for here, there, at in ((CA - 1, CA, CA - 1), (0, ROWS - 1, ROWS - 1)):
        for c in range(3):
            flux = (gains[c] * E / 2) * k_row[at, lay, :] * (u[c, there, lay, :] - u[c, here, lay, :])
            p[0, c, here, lay, :] = p[0, c, here, lay, :] + flux
            p[0, c, there, lay, :] = p[0, c, there, lay, :] - flux
    downward(p_down)
    upward(p_up)
    from_bands([p_down], [p_up])

    sums = {}

    def one_row(j, i):
        up, dn = lax.rem(i + 1, ROWS), lax.rem(i + ROWS - 1, ROWS)
        kr_up, kr_dn, ku, kd, ko, ki = k_row[i], k_row[dn], k_up[i], k_dn[i], k_out[i], k_in[i]
        out = []
        for c in range(3):
            v = p[j, c, i]
            near = ku * pltpu.roll(v, LEV - 1, 0) + kd * pltpu.roll(v, 1, 0)
            near = near + ko * pltpu.roll(v, NR - 1, 1) + ki * pltpu.roll(v, 1, 1)
            near = near + kr_up * p[j, c, up] + kr_dn * p[j, c, dn]
            if c == 2:
                near = near + near
            w = diag[c // 2, i] * v - near
            w = 0.5 * w if j == 0 else w - p[j - 1, c, i]
            p[j + 1, c, i] = w
            out.append(w)
        return out

    for j in range(ITERS):
        pairs = [q for q in PAIRS if q[1] == j + 1 or (j == 0 and q == (0, 0))]

        def own_row(i, acc):
            new = one_row(j, i)
            acc = list(acc)
            for c in range(3):
                w = new[c][0:LAYERS]
                for n, (lo, hi) in enumerate(pairs):
                    a = w if lo == j + 1 else p[lo, c, i, lay, :]
                    d = w if hi == j + 1 else p[hi, c, i, lay, :]
                    acc[n] = acc[n] + a * d
            return tuple(acc)

        totals = lax.fori_loop(0, CA, own_row, tuple(jnp.zeros((LAYERS, NR), jnp.float32) for _ in pairs))
        sums.update(zip(pairs, totals))
        wide = ITERS - 1 - j
        if wide:

            @pl.loop(0, 2 * wide)
            def _(i):
                one_row(j, jnp.where(i < wide, CA + i, ROWS - 1 - (i - wide)))

    gtile[...] = jnp.zeros_like(gtile)
    for n, q in enumerate(PAIRS):
        t = jnp.sum(sums[q], axis=0, keepdims=True)
        gtile[n : n + 1, :] = t[:, 0:128] + t[:, 128:256]

    def reduce_over(group, slots, sends, recvs):
        copies = [
            pltpu.make_async_remote_copy(
                src_ref=gtile,
                dst_ref=slots.at[n],
                send_sem=sends.at[n],
                recv_sem=recvs.at[n],
                device_id=target,
                device_id_type=MESH,
            )
            for n, target in enumerate(group)
        ]
        for copy in copies:
            copy.start()
        for copy in copies:
            copy.wait()
        total = gtile[...]
        for n in range(len(group)):
            total = total + slots[n]
        gtile[...] = total

    reduce_over(group_a, red_a, ra_send, ra_recv)
    reduce_over(group_b, red_b, rb_send, rb_recv)
    reduce_over(group_c, red_c, rc_send, rc_recv)
    g = jnp.broadcast_to(jnp.sum(gtile[...], axis=1, keepdims=True), (16, 128))
    where = {q: n for n, q in enumerate(PAIRS)}
    grams = {q: g[where[q] : where[q] + 1, :] for q in PAIRS}
    xs, rs = coefficients(lambda i, j: grams[(i, j)])
    xs = [jnp.concatenate([v, v], axis=1) for v in xs]
    rs = [jnp.concatenate([v, v], axis=1) for v in rs]

    @pl.loop(0, CA)
    def _(i):
        for c in range(3):
            vs = [p[j, c, i, lay, :] for j in range(ITERS + 1)]
            inc, res = xs[0] * vs[0], rs[0] * vs[0]
            for j in range(1, ITERS):
                inc = inc + xs[j] * vs[j]
            for j in range(1, ITERS + 1):
                res = res + rs[j] * vs[j]
            inc_ref[c, i] = inc
            res_ref[c, i] = res

    @pl.when(jnp.logical_not(low))
    def _():
        force_copy(1).wait_recv()

    force_ref[...] = force_in[0:3, 0:4]

    for slot in range(1, N_BAND):

        @pl.when(b == slot)
        def _():
            pack_copy(slot).wait_send()

    @pl.when(low)
    def _():
        for slot in range(1, N_BAND):
            force_copy(slot).wait_send()

    for copy in (st_first, st_last, u_first, u_last, me_first, me_last, bd_first, bd_last):
        copy.wait_send()

    @pl.when(jnp.logical_not(low))
    def _():
        for copy in (u_down, st_down, me_down, st_rim_down, me_rim_down, p_down):
            copy.wait_send()

    @pl.when(jnp.logical_not(high))
    def _():
        for copy in (u_up, st_up, me_up, st_rim_up, me_rim_up, p_up):
            copy.wait_send()


def per_device(
    given_load,
    displacement,
    mass_coef,
    stiffness,
    bearing_node,
    stick_state,
    slip_prev,
    bearing_old,
    bearing_weight,
):
    f32 = jnp.float32
    vmem, dma = pltpu.VMEM, pltpu.SemaphoreType.DMA
    field = jax.ShapeDtypeStruct((3, CA, LAYERS, NR), f32)
    in_vmem = pl.BlockSpec(memory_space=vmem)
    anywhere = pl.BlockSpec(memory_space=pl.ANY)
    return pl.pallas_call(
        kernel,
        out_shape=(field, field, jax.ShapeDtypeStruct((3, 4), f32)),
        in_specs=[anywhere] * 4 + [in_vmem] * 5,
        out_specs=(in_vmem, in_vmem, in_vmem),
        scratch_shapes=[
            vmem((ROWS, LEV, NR), f32),
            vmem((ROWS, LEV, NR), f32),
            vmem((3, ROWS, LEV, NR), f32),
            vmem((ITERS + 1, 3, ROWS, LEV, NR), f32),
            vmem((ROWS, LEV, NR), f32),
            vmem((ROWS, LEV, NR), f32),
            vmem((ROWS, LEV, NR), f32),
            vmem((ROWS, LEV, NR), f32),
            vmem((ROWS, LEV, NR), f32),
            vmem((2, ROWS, LEV, NR), f32),
            vmem((2, ROWS, NR), f32),
            vmem((3, CA, NR), f32),
            vmem((8, 128), f32),
            vmem((N_BAND, 8, 128), f32),
            vmem((N_BAND, 8, 128), f32),
            vmem((8, 128), f32),
            vmem((16, 128), f32),
            vmem((7, 16, 128), f32),
            vmem((NX - 1, 16, 128), f32),
            vmem((NZ - 1, 16, 128), f32),
            dma((4,)),
            dma((22,)),
            dma((22,)),
            dma((N_BAND,)),
            dma((N_BAND,)),
            dma((N_BAND,)),
            dma((1,)),
            dma((7,)),
            dma((7,)),
            dma((NX - 1,)),
            dma((NX - 1,)),
            dma((NZ - 1,)),
            dma((NZ - 1,)),
        ],
        compiler_params=pltpu.CompilerParams(
            collective_id=0, has_side_effects=True, vmem_limit_bytes=40 * 1024 * 1024
        ),
        name="newton_step",
    )(
        given_load,
        displacement,
        mass_coef,
        stiffness,
        bearing_node.reshape(1, 4),
        stick_state.reshape(1, 4),
        slip_prev,
        bearing_old,
        bearing_weight.reshape(1, 4),
    )


def solution(mesh):
    return jax.shard_map(
        per_device,
        mesh=mesh,
        in_specs=(
            P(None, "sector", "band", None),
            P(None, "sector", "band", None),
            P("sector", "band", None),
            P("sector", "band", None),
            P(("sector", "band")),
            P(("sector", "band")),
            P(None, ("sector", "band")),
            P(None, ("sector", "band")),
            P(("sector", "band")),
        ),
        out_specs=(
            P(None, "sector", "band", None),
            P(None, "sector", "band", None),
            P(None, ("sector", "band")),
        ),
        check_vma=False,
    )
```

time: 665 us -> 63.5 us (0.10)
  blocking collectives: 551 us -> 0 us
  starting transfers between devices: 79.7 us -> 0 us
  Pallas kernels: 0 us -> 56 us
  other arithmetic: 10.7 us -> 0 us
  between operations: 10.6 us -> 0.69 us
  waiting for transfers between devices: 6.91 us -> 0 us
    psum x9 -> x0, blocking collectives: 551 us -> none  [the longest x4 297 us: residual_squares(): return lax.psum(jnp.sum(residual * residual), ('sector', 'band'))]
    ppermute x24 -> x0, starting transfers between devices: 79.7 us -> none  [the longest x12 52.2 us: padded(): after = lax.ppermute(leading, axis, down)]
    pallas_call x0 -> x1, Pallas kernels: none -> 56 us  [per_device(): pl.pallas_call(kernel, out_shape=(field, field, jax.ShapeDtypeStruct((3,...]
    ppermute x24 -> x0, waiting for transfers between devices: 6.91 us -> none  [the longest x12 6.88 us: padded(): before = lax.ppermute(last, axis, up)]
  transfers between devices with their start and end apart: 24 -> 0, of which waited for: 5 -> 0; matrix products, arithmetic and copies ran while one was open for 1% -> 0% of each run, Pallas kernels for 0% -> 0%
where the time goes in v1:
time: 63.5 us; the launch traced here: 63.3 us
  Pallas kernels  56 us (88%)
  local copies, waits for them, and re-layouts  6.56 us (10%)
  between operations  0.69 us (1%)
    pallas_call x1, Pallas kernels, per_device(): pl.pallas_call(kernel, out_shape=(field, field, jax.ShapeDtypeStruct((3,...  56 us
    unnamed x21, local copies, waits for them, and re-layouts  6.56 us

profile of v1, /device:TPU:1, one launch (start us, length us, event | category | flops | bytes accessed | tf_op | source)
XLA Modules:
  0.0 63.3 jit_solution(13133661735464826113)
XLA Ops:
  0.6 0.0 copy-start.5
  0.6 0.0 copy-start.7
  0.7 0.0 copy-start.8
  0.7 0.0 copy-start.4
  0.7 0.0 copy-start.6
  0.7 0.6 copy-done.5
  1.3 0.0 copy-done.7
  1.3 0.0 copy-done.8
  1.3 0.0 copy-done.4
  1.4 0.0 copy-done.6
  1.4 0.0 copy-start
  1.4 1.0 %copy-done = f32[3,8,16,256]{3,2,1,0:T(8,128)S(1)} copy-done((f32[3,8,16,256]{3,2,1,0:T(8,128)S(1)}, f32[3,8,16,256]{3,2,1,0:T(8,128)}, u32[]{:S(2)}) %copy-start) | copy-done | bytes 393240
  2.4 0.0 copy-start.1
  2.4 1.0 %copy-done.1 = f32[3,8,16,256]{3,2,1,0:T(8,128)S(1)} copy-done((f32[3,8,16,256]{3,2,1,0:T(8,128)S(1)}, f32[3,8,16,256]{3,2,1,0:T(8,128)}, u32[]{:S(2)}) %copy-start.1) | copy-done | bytes 393240
  3.4 0.0 copy-start.2
  3.4 0.9 %copy-done.2 = f32[8,16,256]{2,1,0:T(8,128)S(1)} copy-done((f32[8,16,256]{2,1,0:T(8,128)S(1)}, f32[8,16,256]{2,1,0:T(8,128)}, u32[]{:S(2)}) %copy-start.2) | copy-done | bytes 131096
  4.3 0.0 copy-start.3
  4.3 0.9 %copy-done.3 = f32[8,16,256]{2,1,0:T(8,128)S(1)} copy-done((f32[8,16,256]{2,1,0:T(8,128)S(1)}, f32[8,16,256]{2,1,0:T(8,128)}, u32[]{:S(2)}) %copy-start.3) | copy-done | bytes 131096
  5.2 56.0 %newton_step.1 = (f32[3,8,16,256]{3,2,1,0:T(8,128)S(1)}, f32[3,8,16,256]{3,2,1,0:T(8,128)S(1)}, f32[3,4]{1,0:T(4,128)S(1)}) custom-call(f32[3,8,16,256]{3,2,1,0:T(8,128)S(1)} %copy-done, f32[3,8,16,256]{3,2,1,0:T(8,128)S(1)} %copy-done.1, f32[8,16,256]{2,1,0:T(8,128)S(1)} %copy-done.2, f32[8,16,256]{2,1,0:T(8,128)S(1)} %copy-done.3, s32[1,4]{1,0:T(1,128)S(1)} %bitcast.3, ...), custom_call_target="tpu_custom_call" | custom-call | tf_op jit(solution)/shard_map/newton_step/pallas_call | solution.py:570
  61.2 0.7 %copy.15 = f32[3,8,16,256]{3,2,1,0:T(8,128)} copy(f32[3,8,16,256]{3,2,1,0:T(8,128)S(1)} %get-tuple-element.6) | data formatting | bytes 786432
  62.0 0.7 %copy.16 = f32[3,8,16,256]{3,2,1,0:T(8,128)} copy(f32[3,8,16,256]{3,2,1,0:T(8,128)S(1)} %get-tuple-element.7) | data formatting | bytes 786432
  62.7 0.6 copy.17
Async XLA Ops:
  0.6 0.7 %copy-start.5 = (f32[2,4]{1,0:T(2,128)S(1)}, f32[2,4]{1,0:T(2,128)}, u32[]{:S(2)}) copy-start(f32[2,4]{1,0:T(2,128)} %old_ref.1) | copy-start | bytes 100
  0.6 0.7 %copy-start.7 = (s32[4]{0:T(128)S(1)}, s32[4]{0:T(128)}, u32[]{:S(2)}) copy-start(s32[4]{0:T(128)} %param.14) | copy-start | bytes 52
  0.7 0.7 %copy-start.8 = (f32[4]{0:T(128)S(1)}, f32[4]{0:T(128)}, u32[]{:S(2)}) copy-start(f32[4]{0:T(128)} %param.17) | copy-start | bytes 52
  0.7 0.7 %copy-start.4 = (f32[2,4]{1,0:T(2,128)S(1)}, f32[2,4]{1,0:T(2,128)}, u32[]{:S(2)}) copy-start(f32[2,4]{1,0:T(2,128)} %slip_ref.1) | copy-start | bytes 100
  0.7 0.7 %copy-start.6 = (s32[4]{0:T(128)S(1)}, s32[4]{0:T(128)}, u32[]{:S(2)}) copy-start(s32[4]{0:T(128)} %param.13) | copy-start | bytes 52
  1.4 1.0 %copy-start = (f32[3,8,16,256]{3,2,1,0:T(8,128)S(1)}, f32[3,8,16,256]{3,2,1,0:T(8,128)}, u32[]{:S(2)}) copy-start(f32[3,8,16,256]{3,2,1,0:T(8,128)} %load_hbm.1) | copy-start | bytes 1179652
  2.4 1.0 %copy-start.1 = (f32[3,8,16,256]{3,2,1,0:T(8,128)S(1)}, f32[3,8,16,256]{3,2,1,0:T(8,128)}, u32[]{:S(2)}) copy-start(f32[3,8,16,256]{3,2,1,0:T(8,128)} %disp_hbm.1) | copy-start | bytes 1179652
  3.4 0.9 %copy-start.2 = (f32[8,16,256]{2,1,0:T(8,128)S(1)}, f32[8,16,256]{2,1,0:T(8,128)}, u32[]{:S(2)}) copy-start(f32[8,16,256]{2,1,0:T(8,128)} %mass_hbm.1) | copy-start | bytes 393220
  4.3 0.9 %copy-start.3 = (f32[8,16,256]{2,1,0:T(8,128)S(1)}, f32[8,16,256]{2,1,0:T(8,128)}, u32[]{:S(2)}) copy-start(f32[8,16,256]{2,1,0:T(8,128)} %stiff_hbm.1) | copy-start | bytes 393220

commit v2 on v1

v2 whole, which is shorter than its diff:
```python
import functools

import jax
import jax.numpy as jnp
from jax import lax
from jax.experimental import pallas as pl
from jax.experimental.pallas import tpu as pltpu
from jax.sharding import PartitionSpec as P

ITERS = 4
K_STICK = 4.0
K_VERT = 8.0
MU_FAST = 0.15
MU_SLOW = 0.04
RATE_GAIN = 2.0
RATE_DECAY = 2.0
V_FLOOR = 0.05
HIGHEST = lax.Precision.HIGHEST
MESH = pl.DeviceIdType.MESH

CA = 8
LAYERS = 16
NR = 256
DEPTH = 4
ROWS = CA + 2 * DEPTH
LEV = LAYERS + 2 * DEPTH
N_SECTOR = 64
N_BAND = 4
NX = 4
NZ = 8
PAIRS = [(0, 0), (0, 1), (1, 1), (0, 2), (1, 2), (2, 2), (0, 3), (1, 3), (2, 3), (3, 3), (0, 4), (1, 4), (2, 4), (3, 4)]


def coefficients(gram, e):
    def apply(d):
        q = [None] * 5

        def add(k, v):
            q[k] = v if q[k] is None else q[k] + v

        for j, dj in enumerate(d):
            t = e * dj
            add(j, t)
            if j == 0:
                add(1, t)
            else:
                add(j + 1, 0.5 * t)
                add(j - 1, 0.5 * t)
        return [v for v in q if v is not None]

    def inner(a, b):
        total = None
        for i, ai in enumerate(a):
            for j, bj in enumerate(b):
                term = ai * bj * gram(min(i, j), max(i, j))
                total = term if total is None else total + term
        return total

    def padded_add(a, b, scale):
        out = []
        for i in range(max(len(a), len(b))):
            if i >= len(a):
                out.append(scale * b[i])
            elif i >= len(b):
                out.append(a[i])
            else:
                out.append(a[i] + scale * b[i])
        return out

    one = jnp.ones_like(gram(0, 0))
    r, d, x = [one], [one], []
    rr = gram(0, 0)
    for k in range(ITERS):
        q = apply(d)
        alpha = rr / inner(d, q)
        x = padded_add(x, d, alpha)
        r = padded_add(r, q, -alpha)
        if k < ITERS - 1:
            new = inner(r, r)
            d = padded_add(r, d, new / rr)
            rr = new
    return x, r


def kernel(
    load_hbm,
    disp_hbm,
    mass_hbm,
    stiff_hbm,
    node_ref,
    stick_ref,
    slip_ref,
    old_ref,
    weight_ref,
    p,
    coef_ref,
    force_ref,
    st,
    me,
    u,
    k_row,
    k_up,
    k_dn,
    k_in,
    k_out,
    diag,
    bear,
    nodes,
    sticks,
    slips,
    olds,
    weighs,
    pack,
    packs,
    forces,
    force_in,
    early_a,
    early_b,
    late_a,
    late_b,
    load_sem,
    send_sem,
    recv_sem,
    pack_send,
    pack_recv,
    force_send,
    force_recv,
    ra_send,
    ra_recv,
    rb_send,
    rb_recv,
):
    s = lax.axis_index("sector")
    b = lax.axis_index("band")
    z, x, yh = s // 8, lax.rem(s // 2, 4), lax.rem(s, 2)
    s_dn, s_up = lax.rem(s + N_SECTOR - 1, N_SECTOR), lax.rem(s + 1, N_SECTOR)
    low, high = b == 0, b == N_BAND - 1

    group_a = []
    for da in range(2):
        for db in range(4):
            if (da, db) != (0, 0):
                group_a.append(((s // 2) * 2 + lax.rem(yh + da, 2), lax.rem(b + db, 4)))
    group_b = [
        ((lax.rem(z + i, NZ) * 4 + lax.rem(x + j, NX)) * 2 + yh, b)
        for i in range(NZ)
        for j in range(NX)
        if (i, j) != (0, 0)
    ]

    barrier = pltpu.get_barrier_semaphore()
    everyone = [(s_dn, b), (s_up, b)] + group_a + group_b
    for target in everyone:
        pl.semaphore_signal(barrier, inc=1, device_id=target, device_id_type=MESH)

    local = [
        pltpu.make_async_copy(stiff_hbm, st.at[0:CA, 0:LAYERS, :], load_sem.at[0]),
        pltpu.make_async_copy(disp_hbm, u.at[:, 0:CA, 0:LAYERS, :], load_sem.at[1]),
        pltpu.make_async_copy(mass_hbm, me.at[0:CA, 0:LAYERS, :], load_sem.at[2]),
        pltpu.make_async_copy(load_hbm, p.at[0, :, 0:CA, 0:LAYERS, :], load_sem.at[3]),
    ]
    small = [
        pltpu.make_async_copy(src, dst, load_sem.at[4 + n])
        for n, (src, dst) in enumerate(
            ((node_ref, nodes), (stick_ref, sticks), (slip_ref, slips), (old_ref, olds), (weight_ref, weighs))
        )
    ]
    for copy in local + small:
        copy.start()

    def remote(i, src, dst, target):
        return pltpu.make_async_remote_copy(
            src_ref=src,
            dst_ref=dst,
            send_sem=send_sem.at[i],
            recv_sem=recv_sem.at[i],
            device_id=target,
            device_id_type=MESH,
        )

    own, rim = slice(0, CA), slice(CA, ROWS)
    first, last = slice(0, DEPTH), slice(CA - DEPTH, CA)
    after, before = slice(CA, CA + DEPTH), slice(CA + DEPTH, ROWS)
    lay = slice(0, LAYERS)
    bottom, top = slice(0, DEPTH), slice(LAYERS - DEPTH, LAYERS)
    above, below = slice(LAYERS, LAYERS + DEPTH), slice(LAYERS + DEPTH, LEV)

    b_dn, b_up = (s, lax.rem(b + N_BAND - 1, N_BAND)), (s, lax.rem(b + 1, N_BAND))
    t_dn, t_up = (s_dn, b), (s_up, b)

    u_down = remote(8, disp_hbm.at[:, :, 0:1, :], u.at[:, own, LAYERS : LAYERS + 1, :], b_dn)
    u_up = remote(9, disp_hbm.at[:, :, LAYERS - 1 : LAYERS, :], u.at[:, own, LEV - 1 : LEV, :], b_up)
    st_down = remote(6, stiff_hbm.at[:, bottom, :], st.at[own, above, :], b_dn)
    st_up = remote(7, stiff_hbm.at[:, top, :], st.at[own, below, :], b_up)
    me_down = remote(10, mass_hbm.at[:, bottom, :], me.at[own, above, :], b_dn)
    me_up = remote(11, mass_hbm.at[:, top, :], me.at[own, below, :], b_up)
    st_first = remote(0, stiff_hbm.at[first], st.at[after, lay, :], t_dn)
    st_last = remote(1, stiff_hbm.at[last], st.at[before, lay, :], t_up)
    me_first = remote(2, mass_hbm.at[0 : DEPTH - 1], me.at[CA : CA + DEPTH - 1, lay, :], t_dn)
    me_last = remote(3, mass_hbm.at[CA - DEPTH + 1 : CA], me.at[CA + DEPTH + 1 : ROWS, lay, :], t_up)
    u_first = remote(4, disp_hbm.at[:, 0:1], u.at[:, CA : CA + 1, lay, :], t_dn)
    u_last = remote(5, disp_hbm.at[:, CA - 1 : CA], u.at[:, ROWS - 1 : ROWS, lay, :], t_up)
    st_rim_down = remote(12, st.at[rim, bottom, :], st.at[rim, above, :], b_dn)
    st_rim_up = remote(13, st.at[rim, top, :], st.at[rim, below, :], b_up)
    me_rim_down = remote(14, me.at[rim, bottom, :], me.at[rim, above, :], b_dn)
    me_rim_up = remote(15, me.at[rim, top, :], me.at[rim, below, :], b_up)
    bd_first = remote(16, bear.at[:, first, :], bear.at[:, after, :], t_dn)
    bd_last = remote(17, bear.at[:, last, :], bear.at[:, before, :], t_up)
    p_first = remote(18, p.at[0, :, first, lay, :], p.at[0, :, after, lay, :], t_dn)
    p_last = remote(19, p.at[0, :, last, lay, :], p.at[0, :, before, lay, :], t_up)
    p_down = remote(20, p.at[0, :, :, bottom, :], p.at[0, :, :, above, :], b_dn)
    p_up = remote(21, p.at[0, :, :, top, :], p.at[0, :, :, below, :], b_up)

    def pack_copy(slot):
        return pltpu.make_async_remote_copy(
            src_ref=pack,
            dst_ref=packs.at[slot],
            send_sem=pack_send.at[slot],
            recv_sem=pack_recv.at[slot],
            device_id=(s, 0),
            device_id_type=MESH,
        )

    def force_copy(slot):
        return pltpu.make_async_remote_copy(
            src_ref=forces.at[slot],
            dst_ref=force_in,
            send_sem=force_send.at[slot],
            recv_sem=force_recv.at[0],
            device_id=(s, slot),
            device_id_type=MESH,
        )

    def downward(*copies):
        @pl.when(jnp.logical_not(low))
        def _():
            for copy in copies:
                copy.start()

    def upward(*copies):
        @pl.when(jnp.logical_not(high))
        def _():
            for copy in copies:
                copy.start()

    def from_bands(downs, ups):
        @pl.when(jnp.logical_not(high))
        def _():
            for copy in downs:
                copy.wait_recv()

        @pl.when(jnp.logical_not(low))
        def _():
            for copy in ups:
                copy.wait_recv()

    pl.semaphore_wait(barrier, len(everyone))

    downward(u_down, st_down)
    upward(u_up, st_up)
    for copy in (u_first, u_last):
        copy.start()
    @pl.when(low)
    def _():
        st[:, LEV - DEPTH : LEV, :] = jnp.zeros((ROWS, DEPTH, NR), jnp.float32)
        me[:, LEV - DEPTH : LEV, :] = jnp.zeros((ROWS, DEPTH, NR), jnp.float32)
        u[:, 0:CA, LEV - 1 : LEV, :] = jnp.zeros((3, CA, 1, NR), jnp.float32)
        p[0, :, :, LEV - DEPTH : LEV, :] = jnp.zeros((3, ROWS, DEPTH, NR), jnp.float32)

    @pl.when(high)
    def _():
        st[:, LAYERS : LAYERS + DEPTH, :] = jnp.zeros((ROWS, DEPTH, NR), jnp.float32)
        me[:, LAYERS : LAYERS + DEPTH, :] = jnp.zeros((ROWS, DEPTH, NR), jnp.float32)
        u[:, 0:CA, LAYERS : LAYERS + 1, :] = jnp.zeros((3, CA, 1, NR), jnp.float32)
        p[0, :, :, LAYERS : LAYERS + DEPTH, :] = jnp.zeros((3, ROWS, DEPTH, NR), jnp.float32)

    def face(a, c, scale=1.0):
        return (2.0 * scale) * a * c / jnp.maximum(a + c, 0.25)

    def spread_to(group, slots, which, send, recv):
        n = len(group)
        return [
            pltpu.make_async_remote_copy(
                src_ref=slots.at[n : n + 1, :],
                dst_ref=slots.at[k : k + 1, :],
                send_sem=send.at[which, k],
                recv_sem=recv.at[which, k],
                device_id=target,
                device_id_type=MESH,
            )
            for k, target in enumerate(group)
        ]

    def send_row(row, group, slots, which, send, recv):
        slots[len(group) : len(group) + 1, :] = row
        copies = spread_to(group, slots, which, send, recv)
        for copy in copies:
            copy.start()
        return copies

    def received(copies, slots):
        for copy in copies:
            copy.wait()
        return jnp.sum(slots[...], axis=0, keepdims=True)

    local[0].wait()
    local[2].wait()
    k_row[0, lay, :] = face(st[0, lay, :], st[1, lay, :])

    def powers_of(i, total):
        k = face(st[i, lay, :], st[i + 1, lay, :])
        d = me[i, lay, :] + 6.0 * (k + k_row[i - 1, lay, :])
        k_row[i, lay, :] = k
        d = d * d
        d = d * d
        return total + d * d

    powers = lax.fori_loop(1, CA - 1, powers_of, jnp.zeros((LAYERS, NR), jnp.float32), unroll=True)
    total = jnp.sum(jnp.sum(powers, axis=0, keepdims=True), axis=1, keepdims=True)
    sent = send_row(jnp.broadcast_to(total, (1, 128)), group_a, early_a, 0, ra_send, ra_recv)
    for copy in (st_first, st_last):
        copy.start()
    downward(me_down)
    upward(me_up)
    pack[...] = jnp.zeros_like(pack)
    me[CA + DEPTH - 1 : CA + DEPTH + 1, lay, :] = jnp.zeros((2, LAYERS, NR), jnp.float32)
    for copy in small:
        copy.wait()
    pack[0:1, 0:4] = nodes[...].astype(jnp.float32)
    pack[1:2, 0:4] = sticks[...].astype(jnp.float32)
    pack[2:4, 0:4] = slips[...]
    pack[4:6, 0:4] = olds[...]
    pack[6:7, 0:4] = weighs[...]

    for slot in range(1, N_BAND):

        @pl.when(b == slot)
        def _():
            pack_copy(slot).start()


    lane = lax.broadcasted_iota(jnp.int32, (LEV, NR), 1)

    def conductances_of(i, scale=1.0):
        a = st[i]
        ku = face(a, pltpu.roll(a, LEV - 1, 0), scale)
        ko = jnp.where(lane == NR - 1, 0.0, face(a, pltpu.roll(a, NR - 1, 1), scale))
        k_up[i] = ku
        k_dn[i] = pltpu.roll(ku, 1, 0)
        k_out[i] = ko
        k_in[i] = pltpu.roll(ko, 1, 1)

    from_bands([u_down, st_down], [u_up, st_up])

    @pl.loop(0, CA)
    def _(i):
        conductances_of(i)

    local[1].wait()
    local[3].wait()

    gains = (1.0, 1.0, 2.0)

    @pl.loop(0, CA)
    def _(i):
        up, dn = jnp.minimum(i + 1, CA - 1), jnp.maximum(i - 1, 0)
        kr_up = k_row[jnp.minimum(i, CA - 2), lay, :]
        kr_dn = k_row[dn, lay, :]
        ku, kd, ko, ki = k_up[i, lay, :], k_dn[i, lay, :], k_out[i, lay, :], k_in[i, lay, :]
        m = me[i, lay, :]
        for c in range(3):
            whole = u[c, i]
            v = whole[0:LAYERS]
            above_v = pltpu.roll(whole, LEV - 1, 0)[0:LAYERS]
            below_v = pltpu.roll(whole, 1, 0)[0:LAYERS]
            acc = ku * (above_v - v) + kd * (below_v - v)
            acc = acc + ko * (pltpu.roll(v, NR - 1, 1) - v) + ki * (pltpu.roll(v, 1, 1) - v)
            acc = acc + kr_up * (u[c, up, lay, :] - v) + kr_dn * (u[c, dn, lay, :] - v)
            p[0, c, i, lay, :] = p[0, c, i, lay, :] - m * v + gains[c] * acc
    for copy in (p_first, p_last, me_first, me_last):
        copy.start()
    sent = send_row(received(sent, early_a), group_b, early_b, 0, rb_send, rb_recv)

    @pl.when(low)
    def _():
        packs[0] = pack[...]
        for slot in range(1, N_BAND):
            pack_copy(slot).wait_recv()
        t = packs[0]
        for slot in range(1, N_BAND):
            t = t + pltpu.roll(packs[slot], 4 * slot, 1)
        t = t[:, 0:128]
        node = t[0:1, :].astype(jnp.int32)
        stick = t[1:2, :] > 0.5
        row_of = node // NR
        col_of = lax.rem(node, NR)
        real = lax.broadcasted_iota(jnp.int32, (1, 128), 1) < 4 * N_BAND
        col_hot = jnp.where(
            jnp.logical_and(lax.broadcasted_iota(jnp.int32, (NR, 128), 0) == col_of, real), 1.0, 0.0
        ).astype(jnp.float32)
        row_hot = jnp.where(lax.broadcasted_iota(jnp.int32, (CA, 128), 0) == row_of, 1.0, 0.0).astype(jnp.float32)
        raft = jnp.concatenate([u[c, r, 0:1, :] for c in range(3) for r in range(CA)], axis=0)
        picked = jnp.dot(raft, col_hot, precision=HIGHEST, preferred_element_type=jnp.float32)
        at = [jnp.sum(picked[CA * c : CA * (c + 1)] * row_hot, axis=0, keepdims=True) for c in range(3)]
        trial = [K_STICK * (at[c] - t[2 + c : 3 + c]) for c in range(2)]
        rate = [RATE_GAIN * (at[c] - t[4 + c : 5 + c]) for c in range(2)]
        speed = jnp.sqrt(rate[0] * rate[0] + rate[1] * rate[1] + V_FLOOR * V_FLOOR)
        friction = MU_FAST - (MU_FAST - MU_SLOW) * jnp.exp(-RATE_DECAY * speed)
        capacity = friction * t[6:7]
        magnitude = jnp.sqrt(trial[0] * trial[0] + trial[1] * trial[1])
        largest = jnp.maximum(magnitude, capacity)
        largest = jnp.where(real, largest, 1.0)
        force = [jnp.where(stick, trial[c], capacity * trial[c] / largest) for c in range(2)]
        force = [jnp.where(real, f, 0.0) for f in force + [K_VERT * at[2]]]
        stick_k = jnp.where(jnp.logical_and(stick, real), K_STICK, 0.0)
        vert_k = jnp.where(real, K_VERT, 0.0)
        weights = jnp.concatenate([row_hot * v for v in force + [stick_k, vert_k]], axis=0)
        spread = lax.dot_general(
            weights, col_hot, (((1,), (1,)), ((), ())), precision=HIGHEST, preferred_element_type=jnp.float32
        )
        for n in range(5):
            bear[n, 0:CA] = spread[CA * n : CA * (n + 1)]
        tile = jnp.concatenate(force + [jnp.zeros((5, 128), jnp.float32)], axis=0)
        force_in[...] = tile
        for slot in range(1, N_BAND):
            forces[slot] = pltpu.roll(tile, 128 - 4 * slot, 1)
        for slot in range(1, N_BAND):
            force_copy(slot).start()

    @pl.when(jnp.logical_not(low))
    def _():
        bear[:, 0:CA, :] = jnp.zeros((5, CA, NR), jnp.float32)

    bd_first.start()
    bd_last.start()


    for copy in (st_first, st_last):
        copy.wait_recv()
    downward(st_rim_down)
    upward(st_rim_up)

    for copy in (u_first, u_last):
        copy.wait_recv()
    for copy in (p_first, p_last):
        copy.wait_send()
    for copy in (p_first, p_last):
        copy.wait_recv()
    for here, there in ((CA - 1, CA), (0, ROWS - 1)):
        k = face(st[here, lay, :], st[there, lay, :])
        for c in range(3):
            flux = gains[c] * k * (u[c, there, lay, :] - u[c, here, lay, :])
            p[0, c, here, lay, :] = p[0, c, here, lay, :] + flux
            p[0, c, there, lay, :] = p[0, c, there, lay, :] - flux
    downward(p_down)
    upward(p_up)
    for copy in (me_first, me_last):
        copy.wait_recv()
    downward(me_rim_down)
    upward(me_rim_up)

    mean = received(sent, early_b) * (1.0 / (N_SECTOR * N_BAND * (CA - 2) * LAYERS * NR))
    e128 = jnp.sqrt(jnp.sqrt(jnp.sqrt(mean)))
    scale128 = 2.0 / e128
    scale = jnp.concatenate([scale128, scale128], axis=1)
    from_bands([st_rim_down], [st_rim_up])
    lev = lax.broadcasted_iota(jnp.int32, (LEV, NR), 0)

    @pl.loop(0, ROWS)
    def _(i):
        conductances_of(i, scale)
        k_row[i] = face(st[i], st[lax.rem(i + 1, ROWS)], scale)

    for copy in (bd_first, bd_last):
        copy.wait_recv()

    @pl.when(low)
    def _():
        for c in range(3):
            for i in range(ROWS):
                p[0, c, i, 0:1, :] = p[0, c, i, 0:1, :] - bear[c, i : i + 1, :]

    from_bands([me_down, me_rim_down], [me_up, me_rim_up])

    @pl.loop(0, ROWS)
    def _(i):
        near = k_up[i] + k_dn[i] + k_out[i] + k_in[i] + k_row[i] + k_row[lax.rem(i + ROWS - 1, ROWS)]
        base = scale * me[i] - 2.0
        for h in range(2):
            extra = scale * bear[3 + h, pl.ds(i, 1), :]
            diag[h, i] = base + (h + 1.0) * near + jnp.where(lev == 0, extra, 0.0)

    from_bands([p_down], [p_up])

    sums = {}

    def one_row(j, i, tall=slice(0, LEV)):
        up, dn = lax.rem(i + 1, ROWS), lax.rem(i + ROWS - 1, ROWS)
        kr_up, kr_dn, ku, kd, ko, ki = [
            k[n, tall, :] for k, n in ((k_row, i), (k_row, dn), (k_up, i), (k_dn, i), (k_out, i), (k_in, i))
        ]
        out = []
        for c in range(3):
            whole = p[j, c, i]
            v = whole[tall]
            near = ku * pltpu.roll(whole, LEV - 1, 0)[tall] + kd * pltpu.roll(whole, 1, 0)[tall]
            near = near + ko * pltpu.roll(v, NR - 1, 1) + ki * pltpu.roll(v, 1, 1)
            near = near + kr_up * p[j, c, up, tall, :] + kr_dn * p[j, c, dn, tall, :]
            if c == 2:
                near = near + near
            w = diag[c // 2, i, tall, :] * v - near
            w = 0.5 * w if j == 0 else w - p[j - 1, c, i, tall, :]
            p[j + 1, c, i, tall, :] = w
            out.append(w)
        return out

    for j in range(ITERS):
        pairs = [q for q in PAIRS if q[1] == j + 1 or (j == 0 and q == (0, 0))]

        def own_row(i, acc):
            new = one_row(j, i, lay if j == ITERS - 1 else slice(0, LEV))
            acc = list(acc)
            for c in range(3):
                w = new[c][0:LAYERS]
                for n, (lo, hi) in enumerate(pairs):
                    a = w if lo == j + 1 else p[lo, c, i, lay, :]
                    d = w if hi == j + 1 else p[hi, c, i, lay, :]
                    acc[n] = acc[n] + a * d
            return tuple(acc)

        totals = lax.fori_loop(0, CA, own_row, tuple(jnp.zeros((LAYERS, NR), jnp.float32) for _ in pairs), unroll=2)
        sums.update(zip(pairs, totals))
        wide = ITERS - 1 - j
        if wide:

            @pl.loop(0, 2 * wide, unroll=2)
            def _(i):
                one_row(j, jnp.where(i < wide, CA + i, ROWS - 1 - (i - wide)))

    rows = []
    for q in PAIRS:
        t = jnp.sum(sums[q], axis=0, keepdims=True)
        rows.append(t[:, 0:128] + t[:, 128:256])
    rows = jnp.concatenate(rows + [jnp.zeros((16 - len(PAIRS), 128), jnp.float32)], axis=0)
    eye = lax.broadcasted_iota(jnp.int32, (16, 128), 0) == lax.broadcasted_iota(jnp.int32, (16, 128), 1)
    row = jnp.sum(jnp.where(eye, jnp.sum(rows, axis=1, keepdims=True), 0.0), axis=0, keepdims=True)
    row = received(send_row(row, group_a, late_a, 1, ra_send, ra_recv), late_a)
    row = received(send_row(row, group_b, late_b, 1, rb_send, rb_recv), late_b)
    g = jnp.broadcast_to(jnp.sum(jnp.where(eye, row, 0.0), axis=1, keepdims=True), (16, 128))
    where = {q: n for n, q in enumerate(PAIRS)}
    grams = {q: g[where[q] : where[q] + 1, :] for q in PAIRS}
    xs, rs = coefficients(lambda i, j: grams[(i, j)], e128)
    for n, v in enumerate(xs + rs):
        coef_ref[n : n + 1, :] = v

    @pl.when(jnp.logical_not(low))
    def _():
        force_copy(1).wait_recv()

    force_ref[...] = force_in[...]

    for slot in range(1, N_BAND):

        @pl.when(b == slot)
        def _():
            pack_copy(slot).wait_send()

    @pl.when(low)
    def _():
        for slot in range(1, N_BAND):
            force_copy(slot).wait_send()

    for copy in (st_first, st_last, u_first, u_last, me_first, me_last, bd_first, bd_last):
        copy.wait_send()

    @pl.when(jnp.logical_not(low))
    def _():
        for copy in (u_down, st_down, me_down, st_rim_down, me_rim_down, p_down):
            copy.wait_send()

    @pl.when(jnp.logical_not(high))
    def _():
        for copy in (u_up, st_up, me_up, st_rim_up, me_rim_up, p_up):
            copy.wait_send()


def combine(p, coef, force, inc_hbm, res_hbm, force_hbm, inc, res, out, sems):
    out[...] = force[0:3, 0:4]
    copies = [pltpu.make_async_copy(out, force_hbm, sems.at[0])]
    copies[0].start()
    rows = [jnp.concatenate([coef[n : n + 1, :]] * 2, axis=1) for n in range(2 * ITERS + 1)]
    xs, rs = rows[:ITERS], rows[ITERS:]
    step = CA // 4
    for chunk in range(4):
        span = slice(chunk * step, (chunk + 1) * step)
        for i in range(chunk * step, (chunk + 1) * step):
            for c in range(3):
                vs = [p[j, c, i, 0:LAYERS, :] for j in range(ITERS + 1)]
                a, r = xs[0] * vs[0], rs[0] * vs[0]
                for j in range(1, ITERS):
                    a = a + xs[j] * vs[j]
                for j in range(1, ITERS + 1):
                    r = r + rs[j] * vs[j]
                inc[c, i] = a
                res[c, i] = r
        for n, (src, dst) in enumerate(((inc, inc_hbm), (res, res_hbm))):
            copy = pltpu.make_async_copy(src.at[:, span], dst.at[:, span], sems.at[1 + 2 * chunk + n])
            copy.start()
            copies.append(copy)
    for copy in copies:
        copy.wait()


def per_device(
    given_load,
    displacement,
    mass_coef,
    stiffness,
    bearing_node,
    stick_state,
    slip_prev,
    bearing_old,
    bearing_weight,
):
    f32, i32 = jnp.float32, jnp.int32
    vmem, dma = pltpu.VMEM, pltpu.SemaphoreType.DMA
    field = jax.ShapeDtypeStruct((3, CA, LAYERS, NR), f32)
    in_vmem = pl.BlockSpec(memory_space=vmem)
    in_hbm = pl.BlockSpec(memory_space=pltpu.HBM)
    basis, coef, force = pl.pallas_call(
        kernel,
        out_shape=(
            jax.ShapeDtypeStruct((ITERS + 1, 3, ROWS, LEV, NR), f32),
            jax.ShapeDtypeStruct((16, 128), f32),
            jax.ShapeDtypeStruct((8, 128), f32),
        ),
        in_specs=[in_hbm] * 9,
        out_specs=(in_vmem, in_vmem, in_vmem),
        scratch_shapes=[
            vmem((ROWS, LEV, NR), f32),
            vmem((ROWS, LEV, NR), f32),
            vmem((3, ROWS, LEV, NR), f32),
            vmem((ROWS, LEV, NR), f32),
            vmem((ROWS, LEV, NR), f32),
            vmem((ROWS, LEV, NR), f32),
            vmem((ROWS, LEV, NR), f32),
            vmem((ROWS, LEV, NR), f32),
            vmem((2, ROWS, LEV, NR), f32),
            vmem((5, ROWS, NR), f32),
            vmem((1, 4), i32),
            vmem((1, 4), i32),
            vmem((2, 4), f32),
            vmem((2, 4), f32),
            vmem((1, 4), f32),
            vmem((8, 128), f32),
            vmem((N_BAND, 8, 128), f32),
            vmem((N_BAND, 8, 128), f32),
            vmem((8, 128), f32),
            vmem((8, 128), f32),
            vmem((32, 128), f32),
            vmem((8, 128), f32),
            vmem((32, 128), f32),
            dma((9,)),
            dma((22,)),
            dma((22,)),
            dma((N_BAND,)),
            dma((N_BAND,)),
            dma((N_BAND,)),
            dma((1,)),
            dma((2, 7)),
            dma((2, 7)),
            dma((2, 31)),
            dma((2, 31)),
        ],
        compiler_params=pltpu.CompilerParams(
            collective_id=0, has_side_effects=True, vmem_limit_bytes=32 * 1024 * 1024
        ),
        name="newton_step",
    )(
        *[
            pltpu.with_memory_space_constraint(a, pltpu.HBM)
            for a in (
                given_load,
                displacement,
                mass_coef,
                stiffness,
                bearing_node.reshape(1, 4),
                stick_state.reshape(1, 4),
                slip_prev,
                bearing_old,
                bearing_weight.reshape(1, 4),
            )
        ]
    )
    return pl.pallas_call(
        combine,
        out_shape=(field, field, jax.ShapeDtypeStruct((3, 4), f32)),
        in_specs=[in_vmem] * 3,
        out_specs=(in_hbm, in_hbm, in_hbm),
        scratch_shapes=[
            vmem((3, CA, LAYERS, NR), f32),
            vmem((3, CA, LAYERS, NR), f32),
            vmem((3, 4), f32),
            dma((9,)),
        ],
        compiler_params=pltpu.CompilerParams(vmem_limit_bytes=16 * 1024 * 1024),
        name="combine",
    )(basis, coef, force)


def solution(mesh):
    return jax.shard_map(
        per_device,
        mesh=mesh,
        in_specs=(
            P(None, "sector", "band", None),
            P(None, "sector", "band", None),
            P("sector", "band", None),
            P("sector", "band", None),
            P(("sector", "band")),
            P(("sector", "band")),
            P(None, ("sector", "band")),
            P(None, ("sector", "band")),
            P(("sector", "band")),
        ),
        out_specs=(
            P(None, "sector", "band", None),
            P(None, "sector", "band", None),
            P(None, ("sector", "band")),
        ),
        check_vma=False,
    )
```

time: 63.5 us -> 50.5 us (0.80)
  local copies, waits for them, and re-layouts: 6.56 us -> 0 us
  Pallas kernels: 56 us -> 49.7 us
    unnamed x21 -> x0, local copies, waits for them, and re-layouts: 6.56 us -> none
    pallas_call x1 -> x2, Pallas kernels: 56 us -> 49.7 us  [the longest x1 48.8 us: per_device(): pl.pallas_call(kernel, out_shape=(jax.ShapeDtypeStruct((ITERS + 1, 3, ROW...]
where the time goes in v2:
time: 50.5 us; the launch traced here: 50.4 us
  Pallas kernels  49.7 us (98%)
  between operations  0.64 us (1%)
    pallas_call x1, Pallas kernels, per_device(): pl.pallas_call(kernel, out_shape=(jax.ShapeDtypeStruct((ITERS + 1, 3, ROW...  48.8 us

profile of v2, /device:TPU:1, one launch (start us, length us, event | category | flops | bytes accessed | tf_op | source)
XLA Modules:
  0.0 50.4 jit_solution(17228706576549195604)
XLA Ops:
  0.6 48.8 %newton_step.1 = (f32[5,3,16,24,256]{4,3,2,1,0:T(8,128)S(1)}, f32[16,128]{1,0:T(8,128)S(1)}, f32[8,128]{1,0:T(8,128)S(1)}) custom-call(f32[3,8,16,256]{3,2,1,0:T(8,128)} %load_hbm.1, f32[3,8,16,256]{3,2,1,0:T(8,128)} %disp_hbm.1, f32[8,16,256]{2,1,0:T(8,128)} %mass_hbm.1, f32[8,16,256]{2,1,0:T(8,128)} %stiff_hbm.1, s32[1,4]{1,0:T(1,128)} %bitcast.3, ...), custom_call_target="tpu_custom_call" | custom-call | tf_op jit(solution)/shard_map/newton_step/pallas_call | solution.py:630
  49.4 1.0 %combine.1 = (f32[3,8,16,256]{3,2,1,0:T(8,128)}, f32[3,8,16,256]{3,2,1,0:T(8,128)}, f32[3,4]{1,0:T(4,128)}) custom-call(f32[5,3,16,24,256]{4,3,2,1,0:T(8,128)S(1)} %get-tuple-element.6.p, f32[16,128]{1,0:T(8,128)S(1)} %get-tuple-element.7.coef, f32[8,128]{1,0:T(8,128)S(1)} %get-tuple-element.8.force), custom_call_target="tpu_custom_call" | custom-call | tf_op jit(solution)/shard_map/combine/pallas_call | solution.py:695

commit v3 on v2

--- a/solution.py
+++ b/solution.py
@@ -125,10 +125,7 @@
     pack_recv,
     force_send,
     force_recv,
-    ra_send,
-    ra_recv,
-    rb_send,
-    rb_recv,
+    red_sem,
 ):
     s = lax.axis_index("sector")
     b = lax.axis_index("band")
@@ -136,22 +133,24 @@
     s_dn, s_up = lax.rem(s + N_SECTOR - 1, N_SECTOR), lax.rem(s + 1, N_SECTOR)
     low, high = b == 0, b == N_BAND - 1
 
-    group_a = []
-    for da in range(2):
-        for db in range(4):
-            if (da, db) != (0, 0):
-                group_a.append(((s // 2) * 2 + lax.rem(yh + da, 2), lax.rem(b + db, 4)))
-    group_b = [
-        ((lax.rem(z + i, NZ) * 4 + lax.rem(x + j, NX)) * 2 + yh, b)
-        for i in range(NZ)
-        for j in range(NX)
-        if (i, j) != (0, 0)
-    ]
+    def group_a(n):
+        k = n + 1
+        return ((s // 2) * 2 + lax.rem(yh + k // N_BAND, 2), lax.rem(b + lax.rem(k, N_BAND), N_BAND))
+
+    def group_b(n):
+        k = n + 1
+        return ((lax.rem(z + k // NX, NZ) * NX + lax.rem(x + lax.rem(k, NX), NX)) * 2 + yh, b)
+
+    size_a, size_b = 2 * N_BAND - 1, NZ * NX - 1
 
     barrier = pltpu.get_barrier_semaphore()
-    everyone = [(s_dn, b), (s_up, b)] + group_a + group_b
-    for target in everyone:
+    for target in ((s_dn, b), (s_up, b)):
         pl.semaphore_signal(barrier, inc=1, device_id=target, device_id_type=MESH)
+    for group, size in ((group_a, size_a), (group_b, size_b)):
+
+        @pl.loop(0, size)
+        def _(n):
+            pl.semaphore_signal(barrier, inc=1, device_id=group(n), device_id_type=MESH)
 
     local = [
         pltpu.make_async_copy(stiff_hbm, st.at[0:CA, 0:LAYERS, :], load_sem.at[0]),
@@ -254,7 +253,7 @@
             for copy in ups:
                 copy.wait_recv()
 
-    pl.semaphore_wait(barrier, len(everyone))
+    pl.semaphore_wait(barrier, 2 + size_a + size_b)
 
     downward(u_down, st_down)
     upward(u_up, st_up)
@@ -277,31 +276,26 @@
     def face(a, c, scale=1.0):
         return (2.0 * scale) * a * c / jnp.maximum(a + c, 0.25)
 
-    def spread_to(group, slots, which, send, recv):
-        n = len(group)
-        return [
+    def send_row(row, group, slots, send, recv):
+        n_others = slots.shape[0] - 1
+        slots[n_others] = row
+
+        @pl.loop(0, n_others)
+        def _(n):
             pltpu.make_async_remote_copy(
-                src_ref=slots.at[n : n + 1, :],
-                dst_ref=slots.at[k : k + 1, :],
-                send_sem=send.at[which, k],
-                recv_sem=recv.at[which, k],
-                device_id=target,
+                src_ref=slots.at[n_others],
+                dst_ref=slots.at[n],
+                send_sem=send,
+                recv_sem=recv,
+                device_id=group(n),
                 device_id_type=MESH,
-            )
-            for k, target in enumerate(group)
-        ]
-
-    def send_row(row, group, slots, which, send, recv):
-        slots[len(group) : len(group) + 1, :] = row
-        copies = spread_to(group, slots, which, send, recv)
-        for copy in copies:
-            copy.start()
-        return copies
-
-    def received(copies, slots):
-        for copy in copies:
-            copy.wait()
-        return jnp.sum(slots[...], axis=0, keepdims=True)
+            ).start()
+
+    def received(slots, send, recv):
+        others = slots.at[0 : slots.shape[0] - 1]
+        pltpu.make_async_copy(others, others, recv).wait()
+        pltpu.make_async_copy(others, others, send).wait()
+        return jnp.sum(slots[...], axis=0)
 
     local[0].wait()
     local[2].wait()
@@ -317,7 +311,7 @@
 
     powers = lax.fori_loop(1, CA - 1, powers_of, jnp.zeros((LAYERS, NR), jnp.float32), unroll=True)
     total = jnp.sum(jnp.sum(powers, axis=0, keepdims=True), axis=1, keepdims=True)
-    sent = send_row(jnp.broadcast_to(total, (1, 128)), group_a, early_a, 0, ra_send, ra_recv)
+    send_row(jnp.broadcast_to(total, (1, 128)), group_a, early_a, red_sem.at[0], red_sem.at[1])
     for copy in (st_first, st_last):
         copy.start()
     downward(me_down)
@@ -379,7 +373,7 @@
             p[0, c, i, lay, :] = p[0, c, i, lay, :] - m * v + gains[c] * acc
     for copy in (p_first, p_last, me_first, me_last):
         copy.start()
-    sent = send_row(received(sent, early_a), group_b, early_b, 0, rb_send, rb_recv)
+    send_row(received(early_a, red_sem.at[0], red_sem.at[1]), group_b, early_b, red_sem.at[2], red_sem.at[3])
 
     @pl.when(low)
     def _():
@@ -459,7 +453,7 @@
     downward(me_rim_down)
     upward(me_rim_up)
 
-    mean = received(sent, early_b) * (1.0 / (N_SECTOR * N_BAND * (CA - 2) * LAYERS * NR))
+    mean = received(early_b, red_sem.at[2], red_sem.at[3]) * (1.0 / (N_SECTOR * N_BAND * (CA - 2) * LAYERS * NR))
     e128 = jnp.sqrt(jnp.sqrt(jnp.sqrt(mean)))
     scale128 = 2.0 / e128
     scale = jnp.concatenate([scale128, scale128], axis=1)
@@ -544,8 +538,10 @@
     rows = jnp.concatenate(rows + [jnp.zeros((16 - len(PAIRS), 128), jnp.float32)], axis=0)
     eye = lax.broadcasted_iota(jnp.int32, (16, 128), 0) == lax.broadcasted_iota(jnp.int32, (16, 128), 1)
     row = jnp.sum(jnp.where(eye, jnp.sum(rows, axis=1, keepdims=True), 0.0), axis=0, keepdims=True)
-    row = received(send_row(row, group_a, late_a, 1, ra_send, ra_recv), late_a)
-    row = received(send_row(row, group_b, late_b, 1, rb_send, rb_recv), late_b)
+    send_row(row, group_a, late_a, red_sem.at[4], red_sem.at[5])
+    row = received(late_a, red_sem.at[4], red_sem.at[5])
+    send_row(row, group_b, late_b, red_sem.at[6], red_sem.at[7])
+    row = received(late_b, red_sem.at[6], red_sem.at[7])
     g = jnp.broadcast_to(jnp.sum(jnp.where(eye, row, 0.0), axis=1, keepdims=True), (16, 128))
     where = {q: n for n, q in enumerate(PAIRS)}
     grams = {q: g[where[q] : where[q] + 1, :] for q in PAIRS}
@@ -656,10 +652,10 @@
             vmem((N_BAND, 8, 128), f32),
             vmem((N_BAND, 8, 128), f32),
             vmem((8, 128), f32),
-            vmem((8, 128), f32),
-            vmem((32, 128), f32),
-            vmem((8, 128), f32),
-            vmem((32, 128), f32),
+            vmem((8, 1, 128), f32),
+            vmem((32, 1, 128), f32),
+            vmem((8, 1, 128), f32),
+            vmem((32, 1, 128), f32),
             dma((9,)),
             dma((22,)),
             dma((22,)),
@@ -667,10 +663,7 @@
             dma((N_BAND,)),
             dma((N_BAND,)),
             dma((1,)),
-            dma((2, 7)),
-            dma((2, 7)),
-            dma((2, 31)),
-            dma((2, 31)),
+            dma((8,)),
         ],
         compiler_params=pltpu.CompilerParams(
             collective_id=0, has_side_effects=True, vmem_limit_bytes=32 * 1024 * 1024

time: 50.5 us -> 49.7 us (0.984)
  Pallas kernels: 49.7 us -> 49 us
    pallas_call x1, Pallas kernels: 48.8 us -> 48 us  [per_device(): pl.pallas_call(kernel, out_shape=(jax.ShapeDtypeStruct((ITERS + 1, 3, ROW...]
where the time goes in v3:
time: 49.7 us; the launch traced here: 49.6 us
  Pallas kernels  49 us (99%)
  between operations  0.64 us (1%)
    pallas_call x1, Pallas kernels, per_device(): pl.pallas_call(kernel, out_shape=(jax.ShapeDtypeStruct((ITERS + 1, 3, ROW...  48 us

profile of v3, /device:TPU:1, one launch (start us, length us, event | category | flops | bytes accessed | tf_op | source)
XLA Modules:
  0.0 49.6 jit_solution(2597574895653414281)
XLA Ops:
  0.6 48.0 %newton_step.1 = (f32[5,3,16,24,256]{4,3,2,1,0:T(8,128)S(1)}, f32[16,128]{1,0:T(8,128)S(1)}, f32[8,128]{1,0:T(8,128)S(1)}) custom-call(f32[3,8,16,256]{3,2,1,0:T(8,128)} %load_hbm.1, f32[3,8,16,256]{3,2,1,0:T(8,128)} %disp_hbm.1, f32[8,16,256]{2,1,0:T(8,128)} %mass_hbm.1, f32[8,16,256]{2,1,0:T(8,128)} %stiff_hbm.1, s32[1,4]{1,0:T(1,128)} %bitcast.3, ...), custom_call_target="tpu_custom_call" | custom-call | tf_op jit(solution)/shard_map/newton_step/pallas_call | solution.py:626
  48.7 1.0 %combine.1 = (f32[3,8,16,256]{3,2,1,0:T(8,128)}, f32[3,8,16,256]{3,2,1,0:T(8,128)}, f32[3,4]{1,0:T(4,128)}) custom-call(f32[5,3,16,24,256]{4,3,2,1,0:T(8,128)S(1)} %get-tuple-element.6.p, f32[16,128]{1,0:T(8,128)S(1)} %get-tuple-element.7.coef, f32[8,128]{1,0:T(8,128)S(1)} %get-tuple-element.8.force), custom_call_target="tpu_custom_call" | custom-call | tf_op jit(solution)/shard_map/combine/pallas_call | solution.py:688

commit v4 on v3

--- a/solution.py
+++ b/solution.py
@@ -207,8 +207,18 @@
     bd_last = remote(17, bear.at[:, last, :], bear.at[:, before, :], t_up)
     p_first = remote(18, p.at[0, :, first, lay, :], p.at[0, :, after, lay, :], t_dn)
     p_last = remote(19, p.at[0, :, last, lay, :], p.at[0, :, before, lay, :], t_up)
-    p_down = remote(20, p.at[0, :, :, bottom, :], p.at[0, :, :, above, :], b_dn)
-    p_up = remote(21, p.at[0, :, :, top, :], p.at[0, :, :, below, :], b_up)
+    less = DEPTH - 1
+    p_down = [
+        remote(20, p.at[0, :, own, bottom, :], p.at[0, :, own, above, :], b_dn),
+        remote(22, p.at[0, :, CA : CA + less, 0:less, :], p.at[0, :, CA : CA + less, LAYERS : LAYERS + less, :], b_dn),
+        remote(23, p.at[0, :, ROWS - less : ROWS, 0:less, :], p.at[0, :, ROWS - less : ROWS, LAYERS : LAYERS + less, :], b_dn),
+    ]
+    far, low_far = slice(LAYERS - less, LAYERS), slice(LEV - less, LEV)
+    p_up = [
+        remote(21, p.at[0, :, own, top, :], p.at[0, :, own, below, :], b_up),
+        remote(24, p.at[0, :, CA : CA + less, far, :], p.at[0, :, CA : CA + less, low_far, :], b_up),
+        remote(25, p.at[0, :, ROWS - less : ROWS, far, :], p.at[0, :, ROWS - less : ROWS, low_far, :], b_up),
+    ]
 
     def pack_copy(slot):
         return pltpu.make_async_remote_copy(
@@ -253,12 +263,6 @@
             for copy in ups:
                 copy.wait_recv()
 
-    pl.semaphore_wait(barrier, 2 + size_a + size_b)
-
-    downward(u_down, st_down)
-    upward(u_up, st_up)
-    for copy in (u_first, u_last):
-        copy.start()
     @pl.when(low)
     def _():
         st[:, LEV - DEPTH : LEV, :] = jnp.zeros((ROWS, DEPTH, NR), jnp.float32)
@@ -311,7 +315,13 @@
 
     powers = lax.fori_loop(1, CA - 1, powers_of, jnp.zeros((LAYERS, NR), jnp.float32), unroll=True)
     total = jnp.sum(jnp.sum(powers, axis=0, keepdims=True), axis=1, keepdims=True)
+    pl.semaphore_wait(barrier, 2 + size_a + size_b)
+
     send_row(jnp.broadcast_to(total, (1, 128)), group_a, early_a, red_sem.at[0], red_sem.at[1])
+    downward(u_down, st_down)
+    upward(u_up, st_up)
+    for copy in (u_first, u_last):
+        copy.start()
     for copy in (st_first, st_last):
         copy.start()
     downward(me_down)
@@ -446,8 +456,8 @@
             flux = gains[c] * k * (u[c, there, lay, :] - u[c, here, lay, :])
             p[0, c, here, lay, :] = p[0, c, here, lay, :] + flux
             p[0, c, there, lay, :] = p[0, c, there, lay, :] - flux
-    downward(p_down)
-    upward(p_up)
+    downward(*p_down)
+    upward(*p_up)
     for copy in (me_first, me_last):
         copy.wait_recv()
     downward(me_rim_down)
@@ -484,7 +494,7 @@
             extra = scale * bear[3 + h, pl.ds(i, 1), :]
             diag[h, i] = base + (h + 1.0) * near + jnp.where(lev == 0, extra, 0.0)
 
-    from_bands([p_down], [p_up])
+    from_bands(p_down, p_up)
 
     sums = {}
 
@@ -571,12 +581,12 @@
 
     @pl.when(jnp.logical_not(low))
     def _():
-        for copy in (u_down, st_down, me_down, st_rim_down, me_rim_down, p_down):
+        for copy in [u_down, st_down, me_down, st_rim_down, me_rim_down] + p_down:
             copy.wait_send()
 
     @pl.when(jnp.logical_not(high))
     def _():
-        for copy in (u_up, st_up, me_up, st_rim_up, me_rim_up, p_up):
+        for copy in [u_up, st_up, me_up, st_rim_up, me_rim_up] + p_up:
             copy.wait_send()
 
 
@@ -657,8 +667,8 @@
             vmem((8, 1, 128), f32),
             vmem((32, 1, 128), f32),
             dma((9,)),
-            dma((22,)),
-            dma((22,)),
+            dma((26,)),
+            dma((26,)),
             dma((N_BAND,)),
             dma((N_BAND,)),
             dma((N_BAND,)),

time: 49.7 us -> 49.3 us (level)
  no operation moved by 1% of the time
where the time goes in v4:
time: 49.3 us; the launch traced here: 49.2 us
  Pallas kernels  48.6 us (99%)
  between operations  0.64 us (1%)
    pallas_call x1, Pallas kernels, per_device(): pl.pallas_call(kernel, out_shape=(jax.ShapeDtypeStruct((ITERS + 1, 3, ROW...  47.6 us

profile of v4, /device:TPU:1, one launch (start us, length us, event | category | flops | bytes accessed | tf_op | source)
XLA Modules:
  0.0 49.2 jit_solution(15278450905086920150)
XLA Ops:
  0.6 47.6 %newton_step.1 = (f32[5,3,16,24,256]{4,3,2,1,0:T(8,128)S(1)}, f32[16,128]{1,0:T(8,128)S(1)}, f32[8,128]{1,0:T(8,128)S(1)}) custom-call(f32[3,8,16,256]{3,2,1,0:T(8,128)} %load_hbm.1, f32[3,8,16,256]{3,2,1,0:T(8,128)} %disp_hbm.1, f32[8,16,256]{2,1,0:T(8,128)} %mass_hbm.1, f32[8,16,256]{2,1,0:T(8,128)} %stiff_hbm.1, s32[1,4]{1,0:T(1,128)} %bitcast.3, ...), custom_call_target="tpu_custom_call" | custom-call | tf_op jit(solution)/shard_map/newton_step/pallas_call | solution.py:636
  48.3 1.0 %combine.1 = (f32[3,8,16,256]{3,2,1,0:T(8,128)}, f32[3,8,16,256]{3,2,1,0:T(8,128)}, f32[3,4]{1,0:T(4,128)}) custom-call(f32[5,3,16,24,256]{4,3,2,1,0:T(8,128)S(1)} %get-tuple-element.6.p, f32[16,128]{1,0:T(8,128)S(1)} %get-tuple-element.7.coef, f32[8,128]{1,0:T(8,128)S(1)} %get-tuple-element.8.force), custom_call_target="tpu_custom_call" | custom-call | tf_op jit(solution)/shard_map/combine/pallas_call | solution.py:698

commit v5 on v4

--- a/solution.py
+++ b/solution.py
@@ -597,9 +597,11 @@
     rows = [jnp.concatenate([coef[n : n + 1, :]] * 2, axis=1) for n in range(2 * ITERS + 1)]
     xs, rs = rows[:ITERS], rows[ITERS:]
     step = CA // 4
-    for chunk in range(4):
-        span = slice(chunk * step, (chunk + 1) * step)
-        for i in range(chunk * step, (chunk + 1) * step):
+
+    @pl.loop(0, 4)
+    def _(chunk):
+        for k in range(step):
+            i = chunk * step + k
             for c in range(3):
                 vs = [p[j, c, i, 0:LAYERS, :] for j in range(ITERS + 1)]
                 a, r = xs[0] * vs[0], rs[0] * vs[0]
@@ -609,10 +611,12 @@
                     r = r + rs[j] * vs[j]
                 inc[c, i] = a
                 res[c, i] = r
+        span = pl.ds(chunk * step, step)
         for n, (src, dst) in enumerate(((inc, inc_hbm), (res, res_hbm))):
-            copy = pltpu.make_async_copy(src.at[:, span], dst.at[:, span], sems.at[1 + 2 * chunk + n])
-            copy.start()
-            copies.append(copy)
+            pltpu.make_async_copy(src.at[:, span], dst.at[:, span], sems.at[1 + n]).start()
+
+    copies.append(pltpu.make_async_copy(inc, inc_hbm, sems.at[1]))
+    copies.append(pltpu.make_async_copy(res, res_hbm, sems.at[2]))
     for copy in copies:
         copy.wait()
 

time: 49.3 us -> 49.4 us (level)
  no operation moved by 1% of the time
where the time goes in v5:
time: 49.4 us; the launch traced here: 49.2 us
  Pallas kernels  48.6 us (98%)
  between operations  0.64 us (1%)
    pallas_call x1, Pallas kernels, per_device(): pl.pallas_call(kernel, out_shape=(jax.ShapeDtypeStruct((ITERS + 1, 3, ROW...  47.6 us

profile of v5, /device:TPU:1, one launch (start us, length us, event | category | flops | bytes accessed | tf_op | source)
XLA Modules:
  0.0 49.2 jit_solution(6947737182205925630)
XLA Ops:
  0.6 47.6 %newton_step.1 = (f32[5,3,16,24,256]{4,3,2,1,0:T(8,128)S(1)}, f32[16,128]{1,0:T(8,128)S(1)}, f32[8,128]{1,0:T(8,128)S(1)}) custom-call(f32[3,8,16,256]{3,2,1,0:T(8,128)} %load_hbm.1, f32[3,8,16,256]{3,2,1,0:T(8,128)} %disp_hbm.1, f32[8,16,256]{2,1,0:T(8,128)} %mass_hbm.1, f32[8,16,256]{2,1,0:T(8,128)} %stiff_hbm.1, s32[1,4]{1,0:T(1,128)} %bitcast.3, ...), custom_call_target="tpu_custom_call" | custom-call | tf_op jit(solution)/shard_map/newton_step/pallas_call | solution.py:640
  48.3 1.0 %combine.1 = (f32[3,8,16,256]{3,2,1,0:T(8,128)}, f32[3,8,16,256]{3,2,1,0:T(8,128)}, f32[3,4]{1,0:T(4,128)}) custom-call(f32[5,3,16,24,256]{4,3,2,1,0:T(8,128)S(1)} %get-tuple-element.6.p, f32[16,128]{1,0:T(8,128)S(1)} %get-tuple-element.7.coef, f32[8,128]{1,0:T(8,128)S(1)} %get-tuple-element.8.force), custom_call_target="tpu_custom_call" | custom-call | tf_op jit(solution)/shard_map/combine/pallas_call | solution.py:702
